TPU v7x, 32 devices: a whole 2x2x4 slice. The times are simulated.
32 devices in a mesh: outer: 8 (over y, x, core), inner: 4 (over z).
Axes of the slice: x: 2, y: 2, z: 4, core: 2. Of those that a mesh axis runs over, the one named last changes fastest.
Arguments:
- output_grad: bfloat16 [8192, 1024], P(('outer', 'inner')), may hold values from -3 to 3
- expert_ids: int32 [8192, 2], P(('outer', 'inner')), may hold values from 0 to 31, all different within a row; in each aligned block of 256 rows (0 to 255, 256 to 511, ...) at most 24 rows name the same one
- gate_weights: float32 [8192, 2], P(('outer', 'inner')), may hold values from 0.2 to 1
- pre_act: bfloat16 [32, 768, 4096], P(('outer', 'inner')), may hold values from -6 to 6
- w_in: bfloat16 [32, 1024, 4096], P(('outer', 'inner')), may hold values from -0.1875 to 0.1875
- w_out: bfloat16 [32, 4096, 1024], P(('outer', 'inner')), may hold values from -0.09375 to 0.09375
Outputs:
- input_grad: bfloat16 [8192, 1024], P(('outer', 'inner'))
- gate_grad: float32 [8192, 2], P(('outer', 'inner'))
Inputs may be any that keep to these rules, and one draw needn't show every extreme that they name: `expert_ids`: the two experts of a token differ. Among the 256 tokens of one device no expert is named more than 24 times, a bound that some block reaches.
All inputs are finite; a program needn't handle non-finite values.
Results may differ from a plain program's by a relative error of at most 0.013.
Values may be sent and summed in bfloat16 or wider, within the bound.
No kernel may reach another device: no remote copies, remote signals or barrier semaphores. Data moves between devices by JAX's collectives and lax.ppermute only.
A program may use at most 128 MiB of HBM per device.

v0:
```python
import jax
import jax.numpy as jnp
from jax import lax
from jax.sharding import PartitionSpec as P


def send_out(slot_rows, gate_col):
    return (
        lax.all_to_all(slot_rows, ("outer", "inner"), split_axis=0, concat_axis=0, tiled=True),
        lax.all_to_all(
            gate_col.astype(jnp.bfloat16),
            ("outer", "inner"),
            split_axis=0,
            concat_axis=0,
            tiled=True,
        ).astype(gate_col.dtype),
    )


def send_back(slot_rows, gate_col):
    return (
        lax.all_to_all(slot_rows, ("outer", "inner"), split_axis=0, concat_axis=0, tiled=True),
        lax.all_to_all(
            gate_col.astype(jnp.bfloat16),
            ("outer", "inner"),
            split_axis=0,
            concat_axis=0,
            tiled=True,
        ).astype(gate_col.dtype),
    )


def per_device(output_grad, expert_ids, gate_weights, pre_act, w_in, w_out):
    outer_count = lax.axis_size("outer")
    inner_count = lax.axis_size("inner")
    dev_count = outer_count * inner_count
    tok_rows = output_grad.shape[0]
    model_width = output_grad.shape[1]
    cap_rows = pre_act.shape[1]
    per_peer = cap_rows // dev_count
    flat_ids = expert_ids.reshape(-1)
    onehot = (flat_ids[:, None] == lax.iota(jnp.int32, dev_count)[None, :]).astype(jnp.int32)
    earlier = jnp.cumsum(onehot, axis=0) - onehot
    slot_pos = jnp.sum(earlier * onehot, axis=1)
    target = flat_ids * per_peer + slot_pos
    routing = target[None, :] == lax.iota(jnp.int32, dev_count * per_peer)[:, None]
    routing_tok = jnp.any(routing.reshape(dev_count * per_peer, tok_rows, 2), axis=2).astype(
        jnp.bfloat16
    )
    send_rows = jnp.dot(routing_tok, output_grad, preferred_element_type=jnp.float32).astype(
        jnp.bfloat16
    )
    send_rows = send_rows.reshape(dev_count, per_peer, model_width)
    send_gate = jnp.sum(jnp.where(routing, gate_weights.reshape(-1)[None, :], 0.0), axis=1).reshape(
        dev_count, per_peer
    )
    recv_rows, recv_gate = send_out(send_rows, send_gate)
    recv_flat = recv_rows.reshape(cap_rows, model_width)
    gate_flat = recv_gate.reshape(cap_rows)
    pre_rows = pre_act[0]
    upstream = lax.dot_general(
        recv_flat, w_out[0], (((1,), (1,)), ((), ())), preferred_element_type=jnp.float32
    )
    relu_out = jnp.maximum(pre_rows.astype(jnp.float32), 0.0)
    slot_gate = jnp.sum(relu_out * upstream, axis=1)
    hidden_grad = jnp.where(pre_rows > 0, gate_flat[:, None] * upstream, 0.0).astype(jnp.bfloat16)
    row_grad = lax.dot_general(
        hidden_grad, w_in[0], (((1,), (1,)), ((), ())), preferred_element_type=jnp.float32
    ).astype(jnp.bfloat16)
    back_rows, back_gate = send_back(
        row_grad.reshape(dev_count, per_peer, model_width), slot_gate.reshape(dev_count, per_peer)
    )
    picked = jnp.einsum(
        "ce,cd->ed",
        routing.astype(jnp.bfloat16),
        back_rows.reshape(dev_count * per_peer, model_width),
        preferred_element_type=jnp.float32,
    )
    input_grad = jnp.sum(picked.reshape(tok_rows, 2, model_width), axis=1).astype(jnp.bfloat16)
    gate_grad = jnp.sum(jnp.where(routing, back_gate.reshape(-1)[:, None], 0.0), axis=0).reshape(
        tok_rows, 2
    )
    return (input_grad, gate_grad)


def solution(mesh):
    placed = (
        P(("outer", "inner"), None),
        P(("outer", "inner"), None),
        P(("outer", "inner"), None),
        P(("outer", "inner"), None, None),
        P(("outer", "inner"), None, None),
        P(("outer", "inner"), None, None),
    )
    return jax.shard_map(
        per_device,
        mesh=mesh,
        in_specs=placed,
        out_specs=(P(("outer", "inner"), None), P(("outer", "inner"), None)),
        check_vma=False,
    )
```

profile of v0, /device:TPU:1, one launch (start us, length us, event | category | flops | bytes accessed | tf_op | source)
XLA Modules:
  0.0 140.7 jit_solution(8207400415140955783)
XLA Ops:
  0.6 0.0 copy-start
  0.6 0.9 copy.38
  1.5 0.1 reshape.124
  1.7 0.1 eq.65
  1.8 1.2 reduce-window.6
  3.0 0.2 slice_reduce_fusion
  3.3 0.1 fusion.21
  3.4 0.1 reduce_sum.48
  3.5 0.1 copy.41
  3.6 0.7 multiply_add_fusion.1
  4.3 0.3 fusion.14
  4.6 0.0 copy-done
  4.6 0.6 convolution_convert_fusion
  5.2 44.7 %all_to_all.22 = bf16[32,24,1024]{2,1,0:T(8,128)(2,1)S(1)} all-to-all(bf16[32,24,1024]{2,1,0:T(8,128)(2,1)S(1)} %bitcast.53), channel_id=1, replica_groups=mesh['outer'=8,'inner'=4] {'outer','inner'}, dimensions={0} | all-to-all | bytes 3145728 | tf_op jit(solution)/shard_map/all_to_all | solution.py:9
  49.8 0.0 copy-start.1
  49.8 14.2 %fusion = (bf16[768]{0:T(1024)(128)(2,1)S(1)}, f32[768,4096]{1,0:T(8,128)}) fusion(bf16[1,768,4096]{2,1,0:T(8,128)(2,1)} %param.9, bf16[768,1024]{1,0:T(8,128)(2,1)S(1)} %bitcast.56, bf16[1,4096,1024]{2,1,0:T(8,128)(2,1)} %param.11), kind=kOutput, calls=%fused_computation.1 | convolution fusion | flops 6455032832 | bytes 28837376 | tf_op jit(solution)/shard_map/dot_general | solution.py:61
  64.0 0.7 convert_element_type.89
  64.7 3.2 %all-to-all-start.3 = ((bf16[32,1,24]{2,1,0:T(2,128)(2,1)}), bf16[32,1,24]{2,1,0:T(2,128)(2,1)S(1)}, u32[]{:S(2)}, u32[]{:S(2)}) async-start(bf16[32,1,24]{2,1,0:T(2,128)(2,1)} %convert_element_type.89), calls=%async_computation.3 | async-start | bytes 32768 | tf_op jit(solution)/shard_map/all_to_all | solution.py:23
  67.9 0.0 copy-done.1
  67.9 0.1 copy.42
  68.0 0.1 broadcast_in_dim.33
  68.2 6.3 %all-to-all-done.3 = bf16[32,1,24]{2,1,0:T(2,128)(2,1)S(1)} async-done(((bf16[32,1,24]{2,1,0:T(2,128)(2,1)}), bf16[32,1,24]{2,1,0:T(2,128)(2,1)S(1)}, u32[]{:S(2)}, u32[]{:S(2)}) %all-to-all-start.3) | async-done | bytes 1568 | tf_op jit(solution)/shard_map/all_to_all | solution.py:23
  74.5 0.1 convert_reduce_fusion
  74.5 0.1 reshape.132
  74.6 0.6 select_reduce_fusion
  75.2 0.1 convert_element_type.88
  75.3 8.9 %all_to_all.23 = bf16[32,1,24]{2,1,0:T(2,128)(2,1)S(1)} all-to-all(bf16[32,1,24]{2,1,0:T(2,128)(2,1)S(1)} %convert_element_type.88), channel_id=1, replica_groups=mesh['outer'=8,'inner'=4] {'outer','inner'}, dimensions={0} | all-to-all | bytes 3072 | tf_op jit(solution)/shard_map/all_to_all | solution.py:10
  84.1 0.1 convert_reduce_fusion.1
  84.2 0.1 reshape.131
  84.3 14.1 %fusion.8 = bf16[768,1024]{1,0:T(8,128)(2,1)} fusion(bf16[1,1024,4096]{2,1,0:T(8,128)(2,1)} %param.10, f32[768,4096]{1,0:T(8,128)} %get-tuple-element.13, bf16[1,768,4096]{2,1,0:T(8,128)(2,1)} %param.9, f32[768]{0:T(1024)S(1)} %reshape.131), kind=kOutput, calls=%fused_computation.10 | convolution fusion | flops 6455820288 | bytes 28838912 | tf_op jit(solution)/shard_map/dot_general | solution.py:67
  98.3 3.0 %all-to-all-start.2 = ((bf16[32,24,1024]{2,1,0:T(8,128)(2,1)}), bf16[32,24,1024]{2,1,0:T(8,128)(2,1)S(1)}, u32[]{:S(2)}, u32[]{:S(2)}) async-start(bf16[32,24,1024]{2,1,0:T(8,128)(2,1)} %bitcast.55), calls=%async_computation.2 | async-start | bytes 3145728 | tf_op jit(solution)/shard_map/all_to_all | solution.py:22
  101.4 0.1 reshape.130
  101.5 0.7 copy.45
  102.2 36.7 %all-to-all-done.2 = bf16[32,24,1024]{2,1,0:T(8,128)(2,1)S(1)} async-done(((bf16[32,24,1024]{2,1,0:T(8,128)(2,1)}), bf16[32,24,1024]{2,1,0:T(8,128)(2,1)S(1)}, u32[]{:S(2)}, u32[]{:S(2)}) %all-to-all-start.2) | async-done | bytes 1572896 | tf_op jit(solution)/shard_map/all_to_all | solution.py:22
  138.9 1.8 %fusion.15 = bf16[256,1024]{1,0:T(8,128)(2,1)} fusion(bf16[768,1024,1]{1,0,2:T(8,128)(2,1)S(1)} %bitcast.54, s32[256,2]{0,1:T(2,128)S(1)} %multiply_add_fusion.1), kind=kOutput, calls=%fused_computation.20 | convolution fusion | flops 805961728 | bytes 2099200 | tf_op jit(solution)/shard_map/ce,cd->ed/dot_general | solution.py:73
  (4 shorter events, 0.1 us)
Async XLA Ops:
  0.6 3.9 %copy-start = (bf16[256,1024]{1,0:T(8,128)(2,1)S(1)}, bf16[256,1024]{1,0:T(8,128)(2,1)}, u32[]{:S(2)}) copy-start(bf16[256,1024]{1,0:T(8,128)(2,1)} %param.6) | copy-start | bytes 1572868
  49.8 18.0 %copy-start.1 = (f32[256,2]{0,1:T(2,128)S(1)}, f32[256,2]{0,1:T(2,128)}, u32[]{:S(2)}) copy-start(f32[256,2]{0,1:T(2,128)} %param.8) | copy-start | bytes 6148
  64.7 9.8 %all-to-all-start.3 = ((bf16[32,1,24]{2,1,0:T(2,128)(2,1)}), bf16[32,1,24]{2,1,0:T(2,128)(2,1)S(1)}, u32[]{:S(2)}, u32[]{:S(2)}) async-start(bf16[32,1,24]{2,1,0:T(2,128)(2,1)} %convert_element_type.89), calls=%async_computation.3 | async-start | bytes 32768 | tf_op jit(solution)/shard_map/all_to_all | solution.py:23
  98.3 40.5 %all-to-all-start.2 = ((bf16[32,24,1024]{2,1,0:T(8,128)(2,1)}), bf16[32,24,1024]{2,1,0:T(8,128)(2,1)S(1)}, u32[]{:S(2)}, u32[]{:S(2)}) async-start(bf16[32,24,1024]{2,1,0:T(8,128)(2,1)} %bitcast.55), calls=%async_computation.2 | async-start | bytes 3145728 | tf_op jit(solution)/shard_map/all_to_all | solution.py:22
where the time goes:
time: 141 us
  blocking collectives  53.5 us (38%)
  waiting for transfers between devices  43 us (30%)
  matrix products  30.6 us (22%)
  starting transfers between devices  6.18 us (4%)
  local copies, waits for them, and re-layouts  3.65 us (3%)
  other arithmetic  2.96 us (2%)
    all_to_all x1, blocking collectives, send_out(): lax.all_to_all(slot_rows, ('outer', 'inner'), split_axis=0, concat_axis=0...  44.7 us
    all_to_all x1, waiting for transfers between devices, send_back(): lax.all_to_all(slot_rows, ('outer', 'inner'), split_axis=0, concat_axis=0...  36.7 us
    dot_general x1, matrix products, per_device(): lax.dot_general(recv_flat, w_out[0], (((1,), (1,)), ((), ())), preferred_...  14.2 us
    dot_general x1, matrix products, per_device(): lax.dot_general(hidden_grad, w_in[0], (((1,), (1,)), ((), ())), preferred...  14.1 us
    all_to_all x1, blocking collectives, send_out(): lax.all_to_all(gate_col.astype(jnp.bfloat16), ('outer', 'inner'), split_a...  8.87 us
    all_to_all x1, waiting for transfers between devices, send_back(): lax.all_to_all(gate_col.astype(jnp.bfloat16), ('outer', 'inner'), split_a...  6.3 us
    all_to_all x1, starting transfers between devices, send_back(): lax.all_to_all(gate_col.astype(jnp.bfloat16), ('outer', 'inner'), split_a...  3.15 us
    all_to_all x1, starting transfers between devices, send_back(): lax.all_to_all(slot_rows, ('outer', 'inner'), split_axis=0, concat_axis=0...  3.03 us
  transfers between devices with their start and end apart: 2, of which 2 were waited for; matrix products, arithmetic and copies ran while one was open for 1% of the time, Pallas kernels for 0%

commit v1 on v0

v1 whole, which is shorter than its diff:
```python
import functools

import jax
import jax.numpy as jnp
from jax import lax
from jax.experimental import pallas as pl
from jax.experimental.pallas import tpu as pltpu
from jax.sharding import PartitionSpec as P

LANES = 128
SUBLANES = 8
NN = (((1,), (0,)), ((), ()))
NT = (((1,), (1,)), ((), ()))
TN = (((0,), (0,)), ((), ()))


def matmul(a, b, dims):
    return lax.dot_general(a, b, dims, preferred_element_type=jnp.float32)


def targets(ids, experts, per_peer):
    tokens = ids.shape[1]
    which = lax.broadcasted_iota(jnp.int32, (experts, tokens), 0)
    first, second = which == ids[0:1], which == ids[1:2]
    named = jnp.where(first | second, 1.0, 0.0).astype(jnp.bfloat16)
    before = lax.broadcasted_iota(jnp.int32, (tokens, tokens), 0) < lax.broadcasted_iota(
        jnp.int32, (tokens, tokens), 1
    )
    earlier = matmul(named, jnp.where(before, 1.0, 0.0).astype(jnp.bfloat16), NN)
    slot = [
        jnp.sum(jnp.where(mine, earlier, 0.0), axis=0, keepdims=True).astype(jnp.int32)
        for mine in (first, second)
    ]
    return ids[0:1] * per_peer + slot[0], ids[1:2] * per_peer + slot[1]


def route_body(experts, per_peer, ids_ref, tok_ref, send_ref, target_ref):
    one, two = targets(ids_ref[...], experts, per_peer)
    target_ref[0:1, :] = one
    target_ref[1:2, :] = two
    row = lax.broadcasted_iota(jnp.int32, (send_ref.shape[0], ids_ref.shape[1]), 0)
    pick = jnp.where((row == one) | (row == two), 1.0, 0.0).astype(jnp.bfloat16)
    send_ref[...] = matmul(pick, tok_ref[...], NN).astype(jnp.bfloat16)


def route(ids, tokens, experts, per_peer):
    rows, width = experts * per_peer, tokens.shape[1]
    return pl.pallas_call(
        functools.partial(route_body, experts, per_peer),
        out_shape=(
            jax.ShapeDtypeStruct((rows, width), jnp.bfloat16),
            jax.ShapeDtypeStruct(ids.shape, jnp.int32),
        ),
        cost_estimate=pl.CostEstimate(
            flops=2 * rows * tokens.shape[0] * width,
            bytes_accessed=2 * (rows + tokens.shape[0]) * width,
            transcendentals=0,
        ),
        name="route",
    )(ids, tokens)


def expert_body(blocks, packed, x_hbm, p_hbm, wo_hbm, wi_hbm, o_ref, x, p, wo, wi, acc, gsum, sem):
    rows, width = x.shape
    size = wo.shape[1]

    def up(j):
        return pltpu.make_async_copy(wo_hbm.at[pl.ds(j * size, size), :], wo.at[j], sem.at[0, j])

    def pre(j):
        return pltpu.make_async_copy(p_hbm.at[:, pl.ds(j * size, size)], p.at[j], sem.at[1, j])

    def down(j):
        return pltpu.make_async_copy(wi_hbm.at[:, pl.ds(j * size, size)], wi.at[j], sem.at[2, j])

    rows_in = pltpu.make_async_copy(x_hbm, x, sem.at[3, 0])
    rows_in.start()
    for j in range(blocks):
        up(j).start()
        pre(j).start()
        down(j).start()
    rows_in.wait()
    up(0).wait()
    upstream = matmul(x[...], wo[0], NT)
    for j in range(blocks):
        pre(j).wait()
        down(j).wait()
        following = None
        if j + 1 < blocks:
            up(j + 1).wait()
            following = matmul(x[...], wo[j + 1], NT)
        act = p[j].astype(jnp.float32)
        prod = jnp.maximum(act, 0.0) * upstream
        part = prod[:, :LANES]
        for q in range(1, size // LANES):
            part = part + prod[:, q * LANES : (q + 1) * LANES]
        hidden = jnp.where(act > 0, upstream, 0.0).astype(jnp.bfloat16)
        back = matmul(hidden, wi[j], NT)
        if j == 0:
            acc[...] = back
            gsum[...] = part
        else:
            acc[...] += back
            gsum[...] += part
        upstream = following
    dots = jnp.sum(gsum[...], axis=1, keepdims=True)
    high = dots.astype(jnp.bfloat16).astype(jnp.float32)
    low = dots - high
    out = acc[...].astype(jnp.bfloat16)
    if not packed:
        lane = lax.broadcasted_iota(jnp.int32, (rows, LANES), 1)
        o_ref[:, :width] = out
        o_ref[:, width:] = jnp.where(lane == 0, high, jnp.where(lane == 1, low, 0.0)).astype(
            jnp.bfloat16
        )
        return
    peers = o_ref.shape[0]
    groups, cols = rows // peers // SUBLANES, width // LANES
    lane = lax.broadcasted_iota(jnp.int32, (peers, SUBLANES, LANES), 2)
    out = out.reshape(peers, groups, SUBLANES, width)
    high = high.reshape(peers, groups, SUBLANES, 1)
    low = low.reshape(peers, groups, SUBLANES, 1)
    tail = jnp.zeros((peers, SUBLANES, LANES), jnp.float32)
    for r in range(groups):
        tail = jnp.where(lane == 2 * r, high[:, r], tail)
        tail = jnp.where(lane == 2 * r + 1, low[:, r], tail)
        for c in range(cols):
            at = (r * cols + c) * SUBLANES
            o_ref[:, at : at + SUBLANES, :] = out[:, r, :, c * LANES : (c + 1) * LANES]
    o_ref[:, groups * cols * SUBLANES :, :] = tail.astype(jnp.bfloat16)


def expert(x, p, wo, wi, peers, blocks):
    rows, width = x.shape
    hidden = p.shape[1]
    size = hidden // blocks
    per_peer = rows // peers
    packed = per_peer % SUBLANES == 0
    shape = (
        (peers, per_peer * (width // LANES) + SUBLANES, LANES)
        if packed
        else (rows, width + LANES)
    )
    return pl.pallas_call(
        functools.partial(expert_body, blocks, packed),
        out_shape=jax.ShapeDtypeStruct(shape, jnp.bfloat16),
        in_specs=[pl.BlockSpec(memory_space=pl.ANY)] * 4,
        out_specs=pl.BlockSpec(memory_space=pltpu.VMEM),
        scratch_shapes=[
            pltpu.VMEM((rows, width), jnp.bfloat16),
            pltpu.VMEM((blocks, rows, size), jnp.bfloat16),
            pltpu.VMEM((blocks, size, width), jnp.bfloat16),
            pltpu.VMEM((blocks, width, size), jnp.bfloat16),
            pltpu.VMEM((rows, width), jnp.float32),
            pltpu.VMEM((rows, LANES), jnp.float32),
            pltpu.SemaphoreType.DMA((4, blocks)),
        ],
        compiler_params=pltpu.CompilerParams(vmem_limit_bytes=48 << 20),
        cost_estimate=pl.CostEstimate(
            flops=4 * rows * width * hidden,
            bytes_accessed=2 * (rows * hidden + 2 * width * hidden + 2 * rows * width),
            transcendentals=0,
        ),
        name="expert",
    )(x, p, wo, wi)


def combine_body(packed, target_ref, gate_ref, back_ref, grad_ref, dots_ref):
    tokens, width = grad_ref.shape
    if packed:
        peers = back_ref.shape[0]
        cols = width // LANES
        groups = back_ref.shape[1] // SUBLANES // cols
        rows = peers * groups * SUBLANES
    else:
        rows = back_ref.shape[0]
    row = lax.broadcasted_iota(jnp.int32, (rows, tokens), 0)
    hit = [row == target_ref[k : k + 1, :] for k in range(2)]
    weight = jnp.where(
        hit[0], gate_ref[0:1, :], jnp.where(hit[1], gate_ref[1:2, :], 0.0)
    )
    high = weight.astype(jnp.bfloat16)
    low = (weight - high.astype(jnp.float32)).astype(jnp.bfloat16)
    if packed:

        def column(c):
            return jnp.stack(
                [
                    back_ref[:, (r * cols + c) * SUBLANES : (r * cols + c + 1) * SUBLANES, :]
                    for r in range(groups)
                ],
                axis=1,
            ).reshape(rows, LANES)

        tail = back_ref[:, groups * cols * SUBLANES :, :].astype(jnp.float32)
        lane = lax.broadcasted_iota(jnp.int32, tail.shape, 2)
        sums = (
            jnp.stack([jnp.where(lane // 2 == r, tail, 0.0) for r in range(groups)], axis=1)
            .reshape(rows, LANES)
            .astype(jnp.bfloat16)
        )
        for c in range(0, cols, 2):
            part = jnp.concatenate([column(c), column(c + 1)], axis=1)
            grad_ref[:, c * LANES : (c + 2) * LANES] = (
                matmul(high, part, TN) + matmul(low, part, TN)
            ).astype(jnp.bfloat16)
    else:
        part = back_ref[:, :width]
        grad_ref[...] = (matmul(high, part, TN) + matmul(low, part, TN)).astype(jnp.bfloat16)
        sums = back_ref[:, width:]
    for k in range(2):
        pick = jnp.where(hit[k], 1.0, 0.0).astype(jnp.bfloat16)
        dots_ref[k : k + 1, :] = jnp.sum(matmul(sums, pick, TN), axis=0, keepdims=True)


def combine(target, gates, back, width):
    tokens = gates.shape[1]
    packed = back.ndim == 3
    return pl.pallas_call(
        functools.partial(combine_body, packed),
        out_shape=(
            jax.ShapeDtypeStruct((tokens, width), jnp.bfloat16),
            jax.ShapeDtypeStruct(gates.shape, jnp.float32),
        ),
        compiler_params=pltpu.CompilerParams(vmem_limit_bytes=32 << 20),
        name="combine",
    )(target, gates, back)


def per_device(output_grad, expert_ids, gate_weights, pre_act, w_in, w_out):
    axes = ("outer", "inner")
    devices = lax.axis_size("outer") * lax.axis_size("inner")
    width = output_grad.shape[1]
    cap_rows = pre_act.shape[1]
    per_peer = cap_rows // devices

    def exchange(x):
        return lax.all_to_all(x, axes, split_axis=0, concat_axis=0, tiled=True)

    send, target = route(expert_ids.T, output_grad, devices, per_peer)
    received = exchange(send.reshape(devices, per_peer, width)).reshape(cap_rows, width)
    result = expert(received, pre_act[0], w_out[0], w_in[0], devices, 4)
    if result.ndim == 3:
        back = exchange(result)
    else:
        back = exchange(result.reshape(devices, per_peer, -1)).reshape(cap_rows, -1)
    input_grad, gate_grad = combine(target, gate_weights.T, back, width)
    return input_grad, gate_grad.T


def solution(mesh):
    rows = P(("outer", "inner"), None)
    blocks = P(("outer", "inner"), None, None)
    return jax.shard_map(
        per_device,
        mesh=mesh,
        in_specs=(rows, rows, rows, blocks, blocks, blocks),
        out_specs=(rows, rows),
        check_vma=False,
    )
```

time: 141 us -> 109 us (0.77)
  waiting for transfers between devices: 43 us -> 0 us
  blocking collectives: 53.5 us -> 87 us
  matrix products: 30.6 us -> 0 us
  Pallas kernels: 0 us -> 21.2 us
  starting transfers between devices: 6.18 us -> 0 us
  local copies, waits for them, and re-layouts: 3.65 us -> 0.01 us
  other arithmetic: 2.96 us -> 0 us
    all_to_all x2 -> x0, waiting for transfers between devices: 43 us -> none  [the longest x1 36.7 us: send_back(): lax.all_to_all(slot_rows, ('outer', 'inner'), split_axis=0, concat_axis=0...]
    all_to_all x2, blocking collectives: 53.5 us -> 87 us  [exchange(): return lax.all_to_all(x, axes, split_axis=0, concat_axis=0, tiled=True)]
    dot_general x4 -> x0, matrix products: 30.6 us -> none  [the longest x1 14.2 us: per_device(): lax.dot_general(recv_flat, w_out[0], (((1,), (1,)), ((), ())), preferred_...]
    pallas_call x0 -> x3, Pallas kernels: none -> 21.2 us  [the longest x1 16.2 us: expert(): pl.pallas_call(functools.partial(expert_body, blocks, packed), out_shape=...]
    all_to_all x2 -> x0, starting transfers between devices: 6.18 us -> none  [the longest x1 3.15 us: send_back(): lax.all_to_all(gate_col.astype(jnp.bfloat16), ('outer', 'inner'), split_a...]
    unnamed x7 -> x4, local copies, waits for them, and re-layouts: 1.67 us -> 0.01 us
  transfers between devices with their start and end apart: 2 -> 0, of which waited for: 2 -> 0; matrix products, arithmetic and copies ran while one was open for 1% -> 0% of each run, Pallas kernels for 0% -> 0%
where the time goes in v1:
time: 109 us
  blocking collectives  87 us (80%)
  Pallas kernels  21.2 us (19%)
    all_to_all x2, blocking collectives, exchange(): return lax.all_to_all(x, axes, split_axis=0, concat_axis=0, tiled=True)  87 us
    pallas_call x1, Pallas kernels, expert(): pl.pallas_call(functools.partial(expert_body, blocks, packed), out_shape=...  16.2 us
    pallas_call x1, Pallas kernels, route(): pl.pallas_call(functools.partial(route_body, experts, per_peer), out_shap...  2.98 us

profile of v1, /device:TPU:1, one launch (start us, length us, event | category | flops | bytes accessed | tf_op | source)
XLA Modules:
  0.0 108.8 jit_solution(15149114348159822298)
XLA Ops:
  0.6 3.0 %route.1 = (bf16[768,1024]{1,0:T(8,128)(2,1)}, s32[2,256]{1,0:T(2,128)}) custom-call(s32[2,256]{1,0:T(2,128)} %bitcast.14, bf16[256,1024]{1,0:T(8,128)(2,1)} %tok_ref.1), custom_call_target="tpu_custom_call" | custom-call | flops 402653184 | bytes 2097152 | tf_op jit(solution)/shard_map/route/pallas_call | solution.py:48
  3.6 44.9 %all_to_all.10 = bf16[32,24,1024]{2,1,0:T(8,128)(2,1)S(1)} all-to-all(bf16[32,24,1024]{2,1,0:T(8,128)(2,1)} %bitcast.10), channel_id=1, replica_groups=mesh['outer'=8,'inner'=4] {'outer','inner'}, dimensions={0} | all-to-all | bytes 3145728 | tf_op jit(solution)/shard_map/all_to_all | solution.py:238
  48.5 16.2 %expert.1 = bf16[32,200,128]{2,1,0:T(8,128)(2,1)S(1)} custom-call(bf16[768,1024]{1,0:T(8,128)(2,1)S(1)} %bitcast.8, bf16[768,4096]{1,0:T(8,128)(2,1)} %bitcast.13, bf16[4096,1024]{1,0:T(8,128)(2,1)} %bitcast.11, bf16[1024,4096]{1,0:T(8,128)(2,1)} %bitcast.12), custom_call_target="tpu_custom_call" | custom-call | flops 12884901888 | bytes 26214400 | tf_op jit(solution)/shard_map/expert/pallas_call | solution.py:144
  64.7 0.0 copy-start
  64.7 0.0 copy-start.1
  64.8 42.1 %all_to_all.11.back_ref = bf16[32,200,128]{2,1,0:T(8,128)(2,1)S(1)} all-to-all(bf16[32,200,128]{2,1,0:T(8,128)(2,1)S(1)} %expert.1), channel_id=1, replica_groups=mesh['outer'=8,'inner'=4] {'outer','inner'}, dimensions={0} | all-to-all | bytes 3276800 | tf_op jit(solution)/shard_map/all_to_all | solution.py:238
  106.9 0.0 copy-done
  106.9 0.0 copy-done.1
  106.9 2.0 %combine.1 = (bf16[256,1024]{1,0:T(8,128)(2,1)}, f32[2,256]{1,0:T(2,128)}) custom-call(s32[2,256]{1,0:T(2,128)S(1)} %copy-done.1, f32[2,256]{1,0:T(2,128)S(1)} %bitcast.9, bf16[32,200,128]{2,1,0:T(8,128)(2,1)S(1)} %all_to_all.11.back_ref), custom_call_target="tpu_custom_call" | custom-call | tf_op jit(solution)/shard_map/combine/pallas_call | solution.py:219
Async XLA Ops:
  64.7 42.1 %copy-start = (f32[256,2]{0,1:T(2,128)S(1)}, f32[256,2]{0,1:T(2,128)}, u32[]{:S(2)}) copy-start(f32[256,2]{0,1:T(2,128)} %param.8) | copy-start | bytes 6148
  64.7 42.1 %copy-start.1 = (s32[2,256]{1,0:T(2,128)S(1)}, s32[2,256]{1,0:T(2,128)}, u32[]{:S(2)}) copy-start(s32[2,256]{1,0:T(2,128)} %get-tuple-element.6.target_ref) | copy-start | bytes 6148

commit v2 on v1

--- a/solution.py
+++ b/solution.py
@@ -9,6 +9,7 @@
 
 LANES = 128
 SUBLANES = 8
+SMALL = 8 << 20
 NN = (((1,), (0,)), ((), ()))
 NT = (((1,), (1,)), ((), ()))
 TN = (((0,), (0,)), ((), ()))
@@ -18,7 +19,7 @@
     return lax.dot_general(a, b, dims, preferred_element_type=jnp.float32)
 
 
-def targets(ids, experts, per_peer):
+def slots(ids, experts):
     tokens = ids.shape[1]
     which = lax.broadcasted_iota(jnp.int32, (experts, tokens), 0)
     first, second = which == ids[0:1], which == ids[1:2]
@@ -27,26 +28,38 @@
         jnp.int32, (tokens, tokens), 1
     )
     earlier = matmul(named, jnp.where(before, 1.0, 0.0).astype(jnp.bfloat16), NN)
-    slot = [
+    return [
         jnp.sum(jnp.where(mine, earlier, 0.0), axis=0, keepdims=True).astype(jnp.int32)
         for mine in (first, second)
     ]
-    return ids[0:1] * per_peer + slot[0], ids[1:2] * per_peer + slot[1]
-
-
-def route_body(experts, per_peer, ids_ref, tok_ref, send_ref, target_ref):
-    one, two = targets(ids_ref[...], experts, per_peer)
-    target_ref[0:1, :] = one
-    target_ref[1:2, :] = two
-    row = lax.broadcasted_iota(jnp.int32, (send_ref.shape[0], ids_ref.shape[1]), 0)
-    pick = jnp.where((row == one) | (row == two), 1.0, 0.0).astype(jnp.bfloat16)
-    send_ref[...] = matmul(pick, tok_ref[...], NN).astype(jnp.bfloat16)
-
-
-def route(ids, tokens, experts, per_peer):
-    rows, width = experts * per_peer, tokens.shape[1]
+
+
+def pick_rows(ids, slot, rows, per_peer, rest):
+    shift = rest.bit_length() - 1
+    half = lax.axis_index("half")
+    row = lax.broadcasted_iota(jnp.int32, (rows, ids.shape[1]), 0)
+    hits = []
+    for k in range(2):
+        e = ids[k : k + 1]
+        peer = ((e >> (shift + 1)) << shift) | (e & (rest - 1))
+        mine = ((e >> shift) & 1) == half
+        hits.append(row == jnp.where(mine, peer * per_peer + slot[k], -1))
+    return jnp.where(hits[0] | hits[1], 1.0, 0.0).astype(jnp.bfloat16)
+
+
+def route_body(experts, per_peer, rest, ids_ref, tok_ref, send_ref, target_ref):
+    ids = ids_ref[...]
+    slot = slots(ids, experts)
+    for k in range(2):
+        target_ref[k : k + 1, :] = ids[k : k + 1] * per_peer + slot[k]
+    near_pick = pick_rows(ids, slot, send_ref.shape[0], per_peer, rest)
+    send_ref[...] = matmul(near_pick, tok_ref[...], NN).astype(jnp.bfloat16)
+
+
+def route(ids, tokens, experts, per_peer, rest):
+    rows, width = experts // 2 * per_peer, tokens.shape[1]
     return pl.pallas_call(
-        functools.partial(route_body, experts, per_peer),
+        functools.partial(route_body, experts, per_peer, rest),
         out_shape=(
             jax.ShapeDtypeStruct((rows, width), jnp.bfloat16),
             jax.ShapeDtypeStruct(ids.shape, jnp.int32),
@@ -56,19 +69,44 @@
             bytes_accessed=2 * (rows + tokens.shape[0]) * width,
             transcendentals=0,
         ),
+        compiler_params=pltpu.CompilerParams(vmem_limit_bytes=60 << 20),
         name="route",
     )(ids, tokens)
 
 
-def expert_body(blocks, packed, x_hbm, p_hbm, wo_hbm, wi_hbm, o_ref, x, p, wo, wi, acc, gsum, sem):
+def gather_body(experts, per_peer, rest, ids_ref, tok_ref, send_ref):
+    ids = ids_ref[...]
+    pick = pick_rows(ids, slots(ids, experts), send_ref.shape[0], per_peer, rest)
+    send_ref[...] = matmul(pick, tok_ref[...], NN).astype(jnp.bfloat16)
+
+
+def gather(ids, tokens, experts, per_peer, rest):
+    rows, width = experts // 2 * per_peer, tokens.shape[1]
+    return pl.pallas_call(
+        functools.partial(gather_body, experts, per_peer, rest),
+        out_shape=jax.ShapeDtypeStruct((rows, width), jnp.bfloat16),
+        compiler_params=pltpu.CompilerParams(vmem_limit_bytes=SMALL),
+        cost_estimate=pl.CostEstimate(flops=40 * 10**9, bytes_accessed=0, transcendentals=0),
+        name="gather",
+    )(ids, tokens)
+
+
+def expert_body(blocks, packed, far, *refs):
+    x_hbm, p_hbm, wo_hbm, wi_hbm = refs[:4]
+    near_hbm = refs[4] if far else None
+    o_ref, x, p, wo, wi, acc, gsum, sem = refs[4 + far :]
     rows, width = x.shape
     size = wo.shape[1]
+    own = lax.axis_index("half")
+    half = 1 - own if far else own
 
     def up(j):
         return pltpu.make_async_copy(wo_hbm.at[pl.ds(j * size, size), :], wo.at[j], sem.at[0, j])
 
     def pre(j):
-        return pltpu.make_async_copy(p_hbm.at[:, pl.ds(j * size, size)], p.at[j], sem.at[1, j])
+        return pltpu.make_async_copy(
+            p_hbm.at[:, half, :, pl.ds(j * size, size)], p.at[j], sem.at[1, j]
+        )
 
     def down(j):
         return pltpu.make_async_copy(wi_hbm.at[:, pl.ds(j * size, size)], wi.at[j], sem.at[2, j])
@@ -79,6 +117,9 @@
         up(j).start()
         pre(j).start()
         down(j).start()
+    if far:
+        near = pltpu.make_async_copy(near_hbm, o_ref.at[:, own], sem.at[3, 1])
+        near.start()
     rows_in.wait()
     up(0).wait()
     upstream = matmul(x[...], wo[0], NT)
@@ -89,7 +130,7 @@
         if j + 1 < blocks:
             up(j + 1).wait()
             following = matmul(x[...], wo[j + 1], NT)
-        act = p[j].astype(jnp.float32)
+        act = p[j].astype(jnp.float32).reshape(rows, size)
         prod = jnp.maximum(act, 0.0) * upstream
         part = prod[:, :LANES]
         for q in range(1, size // LANES):
@@ -107,14 +148,17 @@
     high = dots.astype(jnp.bfloat16).astype(jnp.float32)
     low = dots - high
     out = acc[...].astype(jnp.bfloat16)
+    if far:
+        near.wait()
+    dst = o_ref.at[:, half] if far else o_ref
     if not packed:
         lane = lax.broadcasted_iota(jnp.int32, (rows, LANES), 1)
-        o_ref[:, :width] = out
-        o_ref[:, width:] = jnp.where(lane == 0, high, jnp.where(lane == 1, low, 0.0)).astype(
-            jnp.bfloat16
-        )
+        tail = jnp.where(lane == 0, high, jnp.where(lane == 1, low, 0.0)).astype(jnp.bfloat16)
+        dst[:, :, :width] = out.reshape(*dst.shape[:2], width)
+        dst[:, :, width:] = tail.reshape(*dst.shape[:2], LANES)
         return
-    peers = o_ref.shape[0]
+    outer, rest = dst.shape[:2]
+    peers = outer * rest
     groups, cols = rows // peers // SUBLANES, width // LANES
     lane = lax.broadcasted_iota(jnp.int32, (peers, SUBLANES, LANES), 2)
     out = out.reshape(peers, groups, SUBLANES, width)
@@ -126,43 +170,53 @@
         tail = jnp.where(lane == 2 * r + 1, low[:, r], tail)
         for c in range(cols):
             at = (r * cols + c) * SUBLANES
-            o_ref[:, at : at + SUBLANES, :] = out[:, r, :, c * LANES : (c + 1) * LANES]
-    o_ref[:, groups * cols * SUBLANES :, :] = tail.astype(jnp.bfloat16)
-
-
-def expert(x, p, wo, wi, peers, blocks):
+            dst[:, :, at : at + SUBLANES, :] = out[:, r, :, c * LANES : (c + 1) * LANES].reshape(
+                outer, rest, SUBLANES, LANES
+            )
+    dst[:, :, groups * cols * SUBLANES :, :] = tail.astype(jnp.bfloat16).reshape(
+        outer, rest, SUBLANES, LANES
+    )
+
+
+def expert(x, p, wo, wi, rest, blocks, near=None):
     rows, width = x.shape
-    hidden = p.shape[1]
+    outer, _, group, hidden = p.shape
     size = hidden // blocks
-    per_peer = rows // peers
+    per_peer = group // rest
+    far = near is not None
     packed = per_peer % SUBLANES == 0
+    both = (2,) if far else ()
     shape = (
-        (peers, per_peer * (width // LANES) + SUBLANES, LANES)
+        (outer, *both, rest, per_peer * (width // LANES) + SUBLANES, LANES)
         if packed
-        else (rows, width + LANES)
-    )
+        else (outer, *both, group, width + LANES)
+    )
+    operands = (x, p, wo, wi) + ((near,) if far else ())
     return pl.pallas_call(
-        functools.partial(expert_body, blocks, packed),
+        functools.partial(expert_body, blocks, packed, int(far)),
         out_shape=jax.ShapeDtypeStruct(shape, jnp.bfloat16),
-        in_specs=[pl.BlockSpec(memory_space=pl.ANY)] * 4,
+        in_specs=[
+            pl.BlockSpec(memory_space=pltpu.HBM if 1 <= i <= 3 else pl.ANY)
+            for i in range(len(operands))
+        ],
         out_specs=pl.BlockSpec(memory_space=pltpu.VMEM),
         scratch_shapes=[
             pltpu.VMEM((rows, width), jnp.bfloat16),
-            pltpu.VMEM((blocks, rows, size), jnp.bfloat16),
+            pltpu.VMEM((blocks, outer, group, size), jnp.bfloat16),
             pltpu.VMEM((blocks, size, width), jnp.bfloat16),
             pltpu.VMEM((blocks, width, size), jnp.bfloat16),
             pltpu.VMEM((rows, width), jnp.float32),
             pltpu.VMEM((rows, LANES), jnp.float32),
             pltpu.SemaphoreType.DMA((4, blocks)),
         ],
-        compiler_params=pltpu.CompilerParams(vmem_limit_bytes=48 << 20),
+        compiler_params=pltpu.CompilerParams(vmem_limit_bytes=50 << 20),
         cost_estimate=pl.CostEstimate(
             flops=4 * rows * width * hidden,
             bytes_accessed=2 * (rows * hidden + 2 * width * hidden + 2 * rows * width),
             transcendentals=0,
         ),
-        name="expert",
-    )(x, p, wo, wi)
+        name="expert_far" if far else "expert_near",
+    )(*operands)
 
 
 def combine_body(packed, target_ref, gate_ref, back_ref, grad_ref, dots_ref):
@@ -222,38 +276,57 @@
             jax.ShapeDtypeStruct((tokens, width), jnp.bfloat16),
             jax.ShapeDtypeStruct(gates.shape, jnp.float32),
         ),
-        compiler_params=pltpu.CompilerParams(vmem_limit_bytes=32 << 20),
+        compiler_params=pltpu.CompilerParams(vmem_limit_bytes=16 << 20),
         name="combine",
     )(target, gates, back)
 
 
 def per_device(output_grad, expert_ids, gate_weights, pre_act, w_in, w_out):
-    axes = ("outer", "inner")
-    devices = lax.axis_size("outer") * lax.axis_size("inner")
+    outer, rest = lax.axis_size("outer"), lax.axis_size("rest")
+    devices = 2 * outer * rest
     width = output_grad.shape[1]
-    cap_rows = pre_act.shape[1]
+    cap_rows, hidden = pre_act.shape[1:]
     per_peer = cap_rows // devices
-
-    def exchange(x):
+    group = rest * per_peer
+    swap = [(0, 1), (1, 0)]
+
+    def exchange(x, axes):
         return lax.all_to_all(x, axes, split_axis=0, concat_axis=0, tiled=True)
 
-    send, target = route(expert_ids.T, output_grad, devices, per_peer)
-    received = exchange(send.reshape(devices, per_peer, width)).reshape(cap_rows, width)
-    result = expert(received, pre_act[0], w_out[0], w_in[0], devices, 4)
-    if result.ndim == 3:
-        back = exchange(result)
+    def to_half(rows):
+        peers = rows.reshape(outer * rest, per_peer, width)
+        return exchange(peers, ("outer", "rest")).reshape(outer * group, width)
+
+    ids = expert_ids.T
+    far_ids = lax.ppermute(ids, "half", swap)
+    far_tokens = lax.ppermute(output_grad, "half", swap)
+    send, target = route(ids, output_grad, devices, per_peer, rest)
+    near_rows = to_half(send)
+    far_rows = to_half(gather(far_ids, far_tokens, devices, per_peer, rest))
+    act = pre_act.reshape(outer, 2, group, hidden)
+    near = expert(near_rows, act, w_out[0], w_in[0], rest, 4)
+    result = expert(far_rows, act, w_out[0], w_in[0], rest, 4, near)
+    if result.ndim == 5:
+        result = result.reshape(devices, *result.shape[3:])
     else:
-        back = exchange(result.reshape(devices, per_peer, -1)).reshape(cap_rows, -1)
+        result = result.reshape(devices, per_peer, -1)
+    back = exchange(result, ("outer", "half", "rest"))
+    if per_peer % SUBLANES:
+        back = back.reshape(cap_rows, -1)
     input_grad, gate_grad = combine(target, gate_weights.T, back, width)
     return input_grad, gate_grad.T
 
 
 def solution(mesh):
-    rows = P(("outer", "inner"), None)
-    blocks = P(("outer", "inner"), None, None)
+    outer, inner = mesh.shape["outer"], mesh.shape["inner"]
+    split = jax.sharding.Mesh(
+        mesh.devices.reshape(outer, 2, inner // 2), ("outer", "half", "rest")
+    )
+    axes = ("outer", "half", "rest")
+    rows, blocks = P(axes, None), P(axes, None, None)
     return jax.shard_map(
         per_device,
-        mesh=mesh,
+        mesh=split,
         in_specs=(rows, rows, rows, blocks, blocks, blocks),
         out_specs=(rows, rows),
         check_vma=False,

time: 109 us -> 106 us (0.972)
  blocking collectives: 87 us -> 44.4 us
  waiting for transfers between devices: 0 us -> 21.4 us
  starting transfers between devices: 0 us -> 13.3 us
  Pallas kernels: 21.2 us -> 25.8 us
    all_to_all x2 -> x1, blocking collectives: 87 us -> 44.4 us  [exchange(): return lax.all_to_all(x, axes, split_axis=0, concat_axis=0, tiled=True)]
    ppermute x0 -> x2, waiting for transfers between devices: none -> 14.7 us  [the longest x1 14.7 us: per_device(): far_ids = lax.ppermute(ids, 'half', swap)]
    all_to_all x0 -> x2, starting transfers between devices: none -> 9.99 us  [exchange(): return lax.all_to_all(x, axes, split_axis=0, concat_axis=0, tiled=True)]
    all_to_all x0 -> x2, waiting for transfers between devices: none -> 6.68 us  [exchange(): return lax.all_to_all(x, axes, split_axis=0, concat_axis=0, tiled=True)]
    pallas_call x2 -> x4, Pallas kernels: 19.2 us -> 23.8 us  [the longest x2 19.9 us: expert(): pl.pallas_call(functools.partial(expert_body, blocks, packed, int(far)),...]
    ppermute x0 -> x2, starting transfers between devices: none -> 3.28 us  [the longest x1 3.2 us: per_device(): far_tokens = lax.ppermute(output_grad, 'half', swap)]
  transfers between devices with their start and end apart: 0 -> 4, of which waited for: 0 -> 3; matrix products, arithmetic and copies ran while one was open for 0% -> 0% of each run, Pallas kernels for 0% -> 13%
where the time goes in v2:
time: 106 us
  blocking collectives  44.4 us (42%)
  Pallas kernels  25.8 us (24%)
  waiting for transfers between devices  21.4 us (20%)
  starting transfers between devices  13.3 us (13%)
    all_to_all x1, blocking collectives, exchange(): return lax.all_to_all(x, axes, split_axis=0, concat_axis=0, tiled=True)  44.4 us
    pallas_call x2, Pallas kernels, expert(): pl.pallas_call(functools.partial(expert_body, blocks, packed, int(far)),...  19.9 us
    ppermute x1, waiting for transfers between devices, per_device(): far_ids = lax.ppermute(ids, 'half', swap)  14.7 us
    all_to_all x2, starting transfers between devices, exchange(): return lax.all_to_all(x, axes, split_axis=0, concat_axis=0, tiled=True)  9.99 us
    all_to_all x2, waiting for transfers between devices, exchange(): return lax.all_to_all(x, axes, split_axis=0, concat_axis=0, tiled=True)  6.68 us
    ppermute x1, starting transfers between devices, per_device(): far_tokens = lax.ppermute(output_grad, 'half', swap)  3.2 us
    pallas_call x1, Pallas kernels, route(): pl.pallas_call(functools.partial(route_body, experts, per_peer, rest), ou...  2.48 us
  transfers between devices with their start and end apart: 4, of which 3 were waited for; matrix products, arithmetic and copies ran while one was open for 0% of the time, Pallas kernels for 13%

profile of v2, /device:TPU:1, one launch (start us, length us, event | category | flops | bytes accessed | tf_op | source)
XLA Modules:
  0.0 105.5 jit_solution(15221778753641484917)
XLA Ops:
  0.6 3.2 %collective-permute-start.1 = (bf16[256,1024]{1,0:T(8,128)(2,1)}, bf16[256,1024]{1,0:T(8,128)(2,1)S(1)}, u32[]{:S(2)}, u32[]{:S(2)}) collective-permute-start(bf16[256,1024]{1,0:T(8,128)(2,1)} %tok_ref.1), channel_id=1, source_target_pairs={{0,2},{2,0},{1,3},{3,1},{4,6},{6,4},{5,7},{7,5},{8,10},{10,8},{9,1... | collective-permute-start | bytes 1572872 | tf_op jit(solution)/shard_map/ppermute | solution.py:302
  3.8 0.1 collective-permute-start
  3.9 2.5 %route.1 = (bf16[384,1024]{1,0:T(8,128)(2,1)}, s32[2,256]{1,0:T(2,128)}) custom-call(s32[2,256]{1,0:T(2,128)} %bitcast.23, bf16[256,1024]{1,0:T(8,128)(2,1)} %tok_ref.1), custom_call_target="tpu_custom_call" | custom-call | flops 201326592 | bytes 1310720 | tf_op jit(solution)/shard_map/route/pallas_call | solution.py:61
  6.4 6.0 %all-to-all-start.1 = ((bf16[16,24,1024]{2,1,0:T(8,128)(2,1)}), bf16[16,24,1024]{2,1,0:T(8,128)(2,1)S(1)}, u32[]{:S(2)}, u32[]{:S(2)}) async-start(bf16[16,24,1024]{2,1,0:T(8,128)(2,1)} %bitcast.21), calls=%async_computation.1 | async-start | bytes 1572864 | tf_op jit(solution)/shard_map/all_to_all | solution.py:294
  12.4 14.7 %collective-permute-done.ids_ref = s32[2,256]{1,0:T(2,128)S(1)} collective-permute-done((s32[2,256]{1,0:T(2,128)}, s32[2,256]{1,0:T(2,128)S(1)}, u32[]{:S(2)}, u32[]{:S(2)}) %collective-permute-start) | collective-permute-done | bytes 2080 | tf_op jit(solution)/shard_map/ppermute | solution.py:301
  27.1 0.0 collective-permute-done.1.tok_ref
  27.1 1.4 %gather.1 = bf16[384,1024]{1,0:T(8,128)(2,1)} custom-call(s32[2,256]{1,0:T(2,128)S(1)} %collective-permute-done.ids_ref, bf16[256,1024]{1,0:T(8,128)(2,1)S(1)} %collective-permute-done.1.tok_ref), custom_call_target="tpu_custom_call" | custom-call | flops 40000000000 | tf_op jit(solution)/shard_map/gather/pallas_call | solution.py:85
  28.5 5.3 %all-to-all-done.1 = bf16[16,24,1024]{2,1,0:T(8,128)(2,1)S(1)} async-done(((bf16[16,24,1024]{2,1,0:T(8,128)(2,1)}), bf16[16,24,1024]{2,1,0:T(8,128)(2,1)S(1)}, u32[]{:S(2)}, u32[]{:S(2)}) %all-to-all-start.1) | async-done | bytes 786464 | tf_op jit(solution)/shard_map/all_to_all | solution.py:294
  33.8 4.0 %all-to-all-start = ((bf16[16,24,1024]{2,1,0:T(8,128)(2,1)}), bf16[16,24,1024]{2,1,0:T(8,128)(2,1)S(1)}, u32[]{:S(2)}, u32[]{:S(2)}) async-start(bf16[16,24,1024]{2,1,0:T(8,128)(2,1)} %bitcast.2), calls=%async_computation | async-start | bytes 1572864 | tf_op jit(solution)/shard_map/all_to_all | solution.py:294
  37.8 9.9 %expert_near.1.refs_4_ = bf16[8,2,200,128]{3,2,1,0:T(8,128)(2,1)S(1)} custom-call(bf16[384,1024]{1,0:T(8,128)(2,1)S(1)} %bitcast.12, bf16[8,2,48,4096]{3,2,1,0:T(8,128)(2,1)} %bitcast.19, bf16[4096,1024]{1,0:T(8,128)(2,1)} %bitcast.15, bf16[1024,4096]{1,0:T(8,128)(2,1)} %bitcast.17), custom_call_target="tpu_custom_call" | custom-call | flops 6442450944 | bytes 21495808 | tf_op jit(solution)/shard_map/expert_near/pallas_call | solution.py:195
  47.7 1.4 %all-to-all-done = bf16[16,24,1024]{2,1,0:T(8,128)(2,1)S(1)} async-done(((bf16[16,24,1024]{2,1,0:T(8,128)(2,1)}), bf16[16,24,1024]{2,1,0:T(8,128)(2,1)S(1)}, u32[]{:S(2)}, u32[]{:S(2)}) %all-to-all-start) | async-done | bytes 786464 | tf_op jit(solution)/shard_map/all_to_all | solution.py:294
  49.1 0.0 copy-start
  49.1 0.0 copy-start.1
  49.1 10.0 %expert_far.1 = bf16[8,2,2,200,128]{4,3,2,1,0:T(8,128)(2,1)S(1)} custom-call(bf16[384,1024]{1,0:T(8,128)(2,1)S(1)} %bitcast.13, bf16[8,2,48,4096]{3,2,1,0:T(8,128)(2,1)} %bitcast.20, bf16[4096,1024]{1,0:T(8,128)(2,1)} %bitcast.16, bf16[1024,4096]{1,0:T(8,128)(2,1)} %bitcast.18, bf16[8,2,200,128]{3,2,1,0:T(8,128)(2,1)S(1)} %expert_near.1.refs_4_), custom_call_target="tpu_custom_call" | custom-call | flops 6442450944 | bytes 21495808 | tf_op jit(solution)/shard_map/expert_far/pallas_call | solution.py:195
  59.1 44.4 %all_to_all.15.back_ref = bf16[32,200,128]{2,1,0:T(8,128)(2,1)S(1)} all-to-all(bf16[32,200,128]{2,1,0:T(8,128)(2,1)S(1)} %bitcast.11), channel_id=1, replica_groups=mesh['outer'=8,'half'=2,'rest'=2] {'outer','half','rest'}, dimensions={0} | all-to-all | bytes 3276800 | tf_op jit(solution)/shard_map/all_to_all | solution.py:294
  103.5 0.0 copy-done
  103.6 0.0 copy-done.1
  103.6 2.0 %combine.1 = (bf16[256,1024]{1,0:T(8,128)(2,1)}, f32[2,256]{1,0:T(2,128)}) custom-call(s32[2,256]{1,0:T(2,128)S(1)} %copy-done.1, f32[2,256]{1,0:T(2,128)S(1)} %bitcast.14, bf16[32,200,128]{2,1,0:T(8,128)(2,1)S(1)} %all_to_all.15.back_ref), custom_call_target="tpu_custom_call" | custom-call | tf_op jit(solution)/shard_map/combine/pallas_call | solution.py:273
Async XLA Ops:
  0.6 26.4 %collective-permute-start.1 = (bf16[256,1024]{1,0:T(8,128)(2,1)}, bf16[256,1024]{1,0:T(8,128)(2,1)S(1)}, u32[]{:S(2)}, u32[]{:S(2)}) collective-permute-start(bf16[256,1024]{1,0:T(8,128)(2,1)} %tok_ref.1), channel_id=1, source_target_pairs={{0,2},{2,0},{1,3},{3,1},{4,6},{6,4},{5,7},{7,5},{8,10},{10,8},{9,1... | collective-permute-start | bytes 1572872 | tf_op jit(solution)/shard_map/ppermute | solution.py:302
  3.8 23.2 %collective-permute-start = (s32[2,256]{1,0:T(2,128)}, s32[2,256]{1,0:T(2,128)S(1)}, u32[]{:S(2)}, u32[]{:S(2)}) collective-permute-start(s32[2,256]{1,0:T(2,128)} %bitcast.22), channel_id=1, source_target_pairs={{0,2},{2,0},{1,3},{3,1},{4,6},{6,4},{5,7},{7,5},{8,10},{10,8},{9,1... | collective-permute-start | bytes 6152 | tf_op jit(solution)/shard_map/ppermute | solution.py:301
  6.4 27.4 %all-to-all-start.1 = ((bf16[16,24,1024]{2,1,0:T(8,128)(2,1)}), bf16[16,24,1024]{2,1,0:T(8,128)(2,1)S(1)}, u32[]{:S(2)}, u32[]{:S(2)}) async-start(bf16[16,24,1024]{2,1,0:T(8,128)(2,1)} %bitcast.21), calls=%async_computation.1 | async-start | bytes 1572864 | tf_op jit(solution)/shard_map/all_to_all | solution.py:294
  33.8 15.3 %all-to-all-start = ((bf16[16,24,1024]{2,1,0:T(8,128)(2,1)}), bf16[16,24,1024]{2,1,0:T(8,128)(2,1)S(1)}, u32[]{:S(2)}, u32[]{:S(2)}) async-start(bf16[16,24,1024]{2,1,0:T(8,128)(2,1)} %bitcast.2), calls=%async_computation | async-start | bytes 1572864 | tf_op jit(solution)/shard_map/all_to_all | solution.py:294
  49.1 54.4 %copy-start = (f32[256,2]{0,1:T(2,128)S(1)}, f32[256,2]{0,1:T(2,128)}, u32[]{:S(2)}) copy-start(f32[256,2]{0,1:T(2,128)} %param.8) | copy-start | bytes 6148
  49.1 54.4 %copy-start.1 = (s32[2,256]{1,0:T(2,128)S(1)}, s32[2,256]{1,0:T(2,128)}, u32[]{:S(2)}) copy-start(s32[2,256]{1,0:T(2,128)} %get-tuple-element.6.target_ref) | copy-start | bytes 6148

commit v3 on v2

--- a/solution.py
+++ b/solution.py
@@ -47,22 +47,24 @@
     return jnp.where(hits[0] | hits[1], 1.0, 0.0).astype(jnp.bfloat16)
 
 
-def route_body(experts, per_peer, rest, ids_ref, tok_ref, send_ref, target_ref):
+def route_body(experts, per_peer, rest, ids_ref, tok_ref, send_ref, target_ref, late_ref):
     ids = ids_ref[...]
     slot = slots(ids, experts)
     for k in range(2):
         target_ref[k : k + 1, :] = ids[k : k + 1] * per_peer + slot[k]
+    late_ref[...] = tok_ref[tok_ref.shape[0] - late_ref.shape[0] :, :]
     near_pick = pick_rows(ids, slot, send_ref.shape[0], per_peer, rest)
     send_ref[...] = matmul(near_pick, tok_ref[...], NN).astype(jnp.bfloat16)
 
 
-def route(ids, tokens, experts, per_peer, rest):
+def route(ids, tokens, early, experts, per_peer, rest):
     rows, width = experts // 2 * per_peer, tokens.shape[1]
     return pl.pallas_call(
         functools.partial(route_body, experts, per_peer, rest),
         out_shape=(
             jax.ShapeDtypeStruct((rows, width), jnp.bfloat16),
             jax.ShapeDtypeStruct(ids.shape, jnp.int32),
+            jax.ShapeDtypeStruct((tokens.shape[0] - early, width), jnp.bfloat16),
         ),
         cost_estimate=pl.CostEstimate(
             flops=2 * rows * tokens.shape[0] * width,
@@ -74,21 +76,44 @@
     )(ids, tokens)
 
 
-def gather_body(experts, per_peer, rest, ids_ref, tok_ref, send_ref):
+def gather_first_body(experts, per_peer, rest, ids_ref, tok_ref, part_ref, pick_ref):
     ids = ids_ref[...]
-    pick = pick_rows(ids, slots(ids, experts), send_ref.shape[0], per_peer, rest)
-    send_ref[...] = matmul(pick, tok_ref[...], NN).astype(jnp.bfloat16)
-
-
-def gather(ids, tokens, experts, per_peer, rest):
+    pick = pick_rows(ids, slots(ids, experts), part_ref.shape[0], per_peer, rest)
+    count = tok_ref.shape[0]
+    part_ref[...] = matmul(pick[:, :count], tok_ref[...], NN).astype(jnp.bfloat16)
+    pick_ref[...] = pick[:, count:]
+
+
+def gather_first(ids, tokens, experts, per_peer, rest):
     rows, width = experts // 2 * per_peer, tokens.shape[1]
     return pl.pallas_call(
-        functools.partial(gather_body, experts, per_peer, rest),
-        out_shape=jax.ShapeDtypeStruct((rows, width), jnp.bfloat16),
+        functools.partial(gather_first_body, experts, per_peer, rest),
+        out_shape=(
+            jax.ShapeDtypeStruct((rows, width), jnp.bfloat16),
+            jax.ShapeDtypeStruct((rows, ids.shape[1] - tokens.shape[0]), jnp.bfloat16),
+        ),
         compiler_params=pltpu.CompilerParams(vmem_limit_bytes=SMALL),
         cost_estimate=pl.CostEstimate(flops=40 * 10**9, bytes_accessed=0, transcendentals=0),
-        name="gather",
+        name="gather_first",
     )(ids, tokens)
+
+
+def gather_last_body(pick_ref, tok_ref, part_ref, send_ref):
+    rows = matmul(pick_ref[...], tok_ref[...], NN) + part_ref[...].astype(jnp.float32)
+    send_ref[...] = rows.astype(jnp.bfloat16)
+
+
+def gather_last(pick, tokens, part):
+    rows, count = pick.shape
+    return pl.pallas_call(
+        gather_last_body,
+        out_shape=jax.ShapeDtypeStruct(part.shape, jnp.bfloat16),
+        compiler_params=pltpu.CompilerParams(vmem_limit_bytes=SMALL),
+        cost_estimate=pl.CostEstimate(
+            flops=2 * rows * count * part.shape[1], bytes_accessed=0, transcendentals=0
+        ),
+        name="gather_last",
+    )(pick, tokens, part)
 
 
 def expert_body(blocks, packed, far, *refs):
@@ -299,10 +324,13 @@
 
     ids = expert_ids.T
     far_ids = lax.ppermute(ids, "half", swap)
-    far_tokens = lax.ppermute(output_grad, "half", swap)
-    send, target = route(ids, output_grad, devices, per_peer, rest)
+    early = output_grad.shape[0] // 2
+    first = lax.ppermute(output_grad[:early], "half", swap)
+    send, target, late = route(ids, output_grad, early, devices, per_peer, rest)
+    second = lax.ppermute(late, "half", swap)
     near_rows = to_half(send)
-    far_rows = to_half(gather(far_ids, far_tokens, devices, per_peer, rest))
+    part, pick = gather_first(far_ids, first, devices, per_peer, rest)
+    far_rows = to_half(gather_last(pick, second, part))
     act = pre_act.reshape(outer, 2, group, hidden)
     near = expert(near_rows, act, w_out[0], w_in[0], rest, 4)
     result = expert(far_rows, act, w_out[0], w_in[0], rest, 4, near)

time: 106 us -> 104 us (0.981)
  waiting for transfers between devices: 21.4 us -> 15.7 us
  starting transfers between devices: 13.3 us -> 17.3 us
  blocking collectives: 44.4 us -> 42.7 us
    ppermute x1, waiting for transfers between devices: 14.7 us -> 0.88 us  [per_device(): far_ids = lax.ppermute(ids, 'half', swap)]
    ppermute x1 -> x2, waiting for transfers between devices: 0.01 us -> 10.9 us  [the longest x1 10.9 us: per_device(): second = lax.ppermute(late, 'half', swap)]
    all_to_all x2, waiting for transfers between devices: 6.68 us -> 3.91 us  [exchange(): return lax.all_to_all(x, axes, split_axis=0, concat_axis=0, tiled=True)]
    ppermute x1 -> x2, starting transfers between devices: 3.2 us -> 5.51 us  [the longest x1 3.2 us: per_device(): first = lax.ppermute(output_grad[:early], 'half', swap)]
    all_to_all x2, starting transfers between devices: 9.99 us -> 11.7 us  [exchange(): return lax.all_to_all(x, axes, split_axis=0, concat_axis=0, tiled=True)]
    all_to_all x1, blocking collectives: 44.4 us -> 42.7 us  [exchange(): return lax.all_to_all(x, axes, split_axis=0, concat_axis=0, tiled=True)]
  transfers between devices with their start and end apart: 4 -> 5, of which waited for: 3 -> 4; matrix products, arithmetic and copies ran while one was open for 0% -> 0% of each run, Pallas kernels for 13% -> 14%
where the time goes in v3:
time: 104 us
  blocking collectives  42.7 us (41%)
  Pallas kernels  26.2 us (25%)
  starting transfers between devices  17.3 us (17%)
  waiting for transfers between devices  15.7 us (15%)
    all_to_all x1, blocking collectives, exchange(): return lax.all_to_all(x, axes, split_axis=0, concat_axis=0, tiled=True)  42.7 us
    pallas_call x2, Pallas kernels, expert(): pl.pallas_call(functools.partial(expert_body, blocks, packed, int(far)),...  19.9 us
    all_to_all x2, starting transfers between devices, exchange(): return lax.all_to_all(x, axes, split_axis=0, concat_axis=0, tiled=True)  11.7 us
    ppermute x1, waiting for transfers between devices, per_device(): second = lax.ppermute(late, 'half', swap)  10.9 us
    all_to_all x2, waiting for transfers between devices, exchange(): return lax.all_to_all(x, axes, split_axis=0, concat_axis=0, tiled=True)  3.91 us
    ppermute x1, starting transfers between devices, per_device(): first = lax.ppermute(output_grad[:early], 'half', swap)  3.2 us
    pallas_call x1, Pallas kernels, route(): pl.pallas_call(functools.partial(route_body, experts, per_peer, rest), ou...  2.51 us
    ppermute x1, starting transfers between devices, per_device(): second = lax.ppermute(late, 'half', swap)  2.31 us
  transfers between devices with their start and end apart: 5, of which 4 were waited for; matrix products, arithmetic and copies ran while one was open for 0% of the time, Pallas kernels for 14%

profile of v3, /device:TPU:1, one launch (start us, length us, event | category | flops | bytes accessed | tf_op | source)
XLA Modules:
  0.0 103.6 jit_solution(4337158754363130355)
XLA Ops:
  0.6 1.0 slice.3
  1.6 3.2 %collective-permute-start.1 = (bf16[128,1024]{1,0:T(8,128)(2,1)S(1)}, bf16[128,1024]{1,0:T(8,128)(2,1)S(1)}, u32[]{:S(2)}, u32[]{:S(2)}) collective-permute-start(bf16[128,1024]{1,0:T(8,128)(2,1)S(1)} %slice.3), channel_id=1, source_target_pairs={{0,2},{2,0},{1,3},{3,1},{4,6},{6,4},{5,7},{7,5},{8,10},{10,8},{9,1... | collective-permute-start | bytes 786440 | tf_op jit(solution)/shard_map/ppermute | solution.py:328
  4.8 0.1 collective-permute-start
  4.9 2.5 %route.1 = (bf16[384,1024]{1,0:T(8,128)(2,1)}, s32[2,256]{1,0:T(2,128)}, bf16[128,1024]{1,0:T(8,128)(2,1)}) custom-call(s32[2,256]{1,0:T(2,128)} %bitcast.23, bf16[256,1024]{1,0:T(8,128)(2,1)} %tok_ref.1), custom_call_target="tpu_custom_call" | custom-call | flops 201326592 | bytes 1310720 | tf_op jit(solution)/shard_map/route/pallas_call | solution.py:62
  7.4 6.0 %all-to-all-start.1 = ((bf16[16,24,1024]{2,1,0:T(8,128)(2,1)}), bf16[16,24,1024]{2,1,0:T(8,128)(2,1)S(1)}, u32[]{:S(2)}, u32[]{:S(2)}) async-start(bf16[16,24,1024]{2,1,0:T(8,128)(2,1)} %bitcast.21), calls=%async_computation.1 | async-start | bytes 1572864 | tf_op jit(solution)/shard_map/all_to_all | solution.py:319
  13.4 2.3 %collective-permute-start.2 = (bf16[128,1024]{1,0:T(8,128)(2,1)}, bf16[128,1024]{1,0:T(8,128)(2,1)S(1)}, u32[]{:S(2)}, u32[]{:S(2)}) collective-permute-start(bf16[128,1024]{1,0:T(8,128)(2,1)} %get-tuple-element.11), channel_id=1, source_target_pairs={{0,2},{2,0},{1,3},{3,1},{4,6},{6,4},{5,7},{7,5},{8,10},{10,8},{9,1... | collective-permute-start | bytes 786440 | tf_op jit(solution)/shard_map/ppermute | solution.py:330
  15.7 0.9 collective-permute-done.ids_ref
  16.5 0.0 collective-permute-done.1.tok_ref
  16.5 0.5 gather_first.1
  17.1 10.9 %collective-permute-done.2.tok_ref = bf16[128,1024]{1,0:T(8,128)(2,1)S(1)} collective-permute-done((bf16[128,1024]{1,0:T(8,128)(2,1)}, bf16[128,1024]{1,0:T(8,128)(2,1)S(1)}, u32[]{:S(2)}, u32[]{:S(2)}) %collective-permute-start.2) | collective-permute-done | bytes 262176 | tf_op jit(solution)/shard_map/ppermute | solution.py:330
  28.0 1.3 %gather_last.1 = bf16[384,1024]{1,0:T(8,128)(2,1)} custom-call(bf16[384,128]{1,0:T(8,128)(2,1)S(1)} %get-tuple-element.10.pick_ref, bf16[128,1024]{1,0:T(8,128)(2,1)S(1)} %collective-permute-done.2.tok_ref, bf16[384,1024]{1,0:T(8,128)(2,1)S(1)} %get-tuple-element.12.part_ref), custom_call_target="tpu_custom_call" | custom-call | flops 100663296 | tf_op jit(solution)/shard_map/gather_last/pallas_call | solution.py:108
  29.3 2.5 %all-to-all-done.1 = bf16[16,24,1024]{2,1,0:T(8,128)(2,1)S(1)} async-done(((bf16[16,24,1024]{2,1,0:T(8,128)(2,1)}), bf16[16,24,1024]{2,1,0:T(8,128)(2,1)S(1)}, u32[]{:S(2)}, u32[]{:S(2)}) %all-to-all-start.1) | async-done | bytes 786464 | tf_op jit(solution)/shard_map/all_to_all | solution.py:319
  31.8 5.8 %all-to-all-start = ((bf16[16,24,1024]{2,1,0:T(8,128)(2,1)}), bf16[16,24,1024]{2,1,0:T(8,128)(2,1)S(1)}, u32[]{:S(2)}, u32[]{:S(2)}) async-start(bf16[16,24,1024]{2,1,0:T(8,128)(2,1)} %bitcast.2), calls=%async_computation | async-start | bytes 1572864 | tf_op jit(solution)/shard_map/all_to_all | solution.py:319
  37.6 9.9 %expert_near.1.refs_4_ = bf16[8,2,200,128]{3,2,1,0:T(8,128)(2,1)S(1)} custom-call(bf16[384,1024]{1,0:T(8,128)(2,1)S(1)} %bitcast.12, bf16[8,2,48,4096]{3,2,1,0:T(8,128)(2,1)} %bitcast.19, bf16[4096,1024]{1,0:T(8,128)(2,1)} %bitcast.15, bf16[1024,4096]{1,0:T(8,128)(2,1)} %bitcast.17), custom_call_target="tpu_custom_call" | custom-call | flops 6442450944 | bytes 21495808 | tf_op jit(solution)/shard_map/expert_near/pallas_call | solution.py:220
  47.5 1.4 %all-to-all-done = bf16[16,24,1024]{2,1,0:T(8,128)(2,1)S(1)} async-done(((bf16[16,24,1024]{2,1,0:T(8,128)(2,1)}), bf16[16,24,1024]{2,1,0:T(8,128)(2,1)S(1)}, u32[]{:S(2)}, u32[]{:S(2)}) %all-to-all-start) | async-done | bytes 786464 | tf_op jit(solution)/shard_map/all_to_all | solution.py:319
  48.9 0.0 copy-start
  48.9 0.0 copy-start.1
  48.9 10.0 %expert_far.1 = bf16[8,2,2,200,128]{4,3,2,1,0:T(8,128)(2,1)S(1)} custom-call(bf16[384,1024]{1,0:T(8,128)(2,1)S(1)} %bitcast.13, bf16[8,2,48,4096]{3,2,1,0:T(8,128)(2,1)} %bitcast.20, bf16[4096,1024]{1,0:T(8,128)(2,1)} %bitcast.16, bf16[1024,4096]{1,0:T(8,128)(2,1)} %bitcast.18, bf16[8,2,200,128]{3,2,1,0:T(8,128)(2,1)S(1)} %expert_near.1.refs_4_), custom_call_target="tpu_custom_call" | custom-call | flops 6442450944 | bytes 21495808 | tf_op jit(solution)/shard_map/expert_far/pallas_call | solution.py:220
  58.9 42.7 %all_to_all.15.back_ref = bf16[32,200,128]{2,1,0:T(8,128)(2,1)S(1)} all-to-all(bf16[32,200,128]{2,1,0:T(8,128)(2,1)S(1)} %bitcast.11), channel_id=1, replica_groups=mesh['outer'=8,'half'=2,'rest'=2] {'outer','half','rest'}, dimensions={0} | all-to-all | bytes 3276800 | tf_op jit(solution)/shard_map/all_to_all | solution.py:319
  101.6 0.0 copy-done
  101.6 0.0 copy-done.1
  101.6 2.0 %combine.1 = (bf16[256,1024]{1,0:T(8,128)(2,1)}, f32[2,256]{1,0:T(2,128)}) custom-call(s32[2,256]{1,0:T(2,128)S(1)} %copy-done.1, f32[2,256]{1,0:T(2,128)S(1)} %bitcast.14, bf16[32,200,128]{2,1,0:T(8,128)(2,1)S(1)} %all_to_all.15.back_ref), custom_call_target="tpu_custom_call" | custom-call | tf_op jit(solution)/shard_map/combine/pallas_call | solution.py:298
Async XLA Ops:
  1.6 14.9 %collective-permute-start.1 = (bf16[128,1024]{1,0:T(8,128)(2,1)S(1)}, bf16[128,1024]{1,0:T(8,128)(2,1)S(1)}, u32[]{:S(2)}, u32[]{:S(2)}) collective-permute-start(bf16[128,1024]{1,0:T(8,128)(2,1)S(1)} %slice.3), channel_id=1, source_target_pairs={{0,2},{2,0},{1,3},{3,1},{4,6},{6,4},{5,7},{7,5},{8,10},{10,8},{9,1... | collective-permute-start | bytes 786440 | tf_op jit(solution)/shard_map/ppermute | solution.py:328
  4.8 11.7 %collective-permute-start = (s32[2,256]{1,0:T(2,128)}, s32[2,256]{1,0:T(2,128)S(1)}, u32[]{:S(2)}, u32[]{:S(2)}) collective-permute-start(s32[2,256]{1,0:T(2,128)} %bitcast.22), channel_id=1, source_target_pairs={{0,2},{2,0},{1,3},{3,1},{4,6},{6,4},{5,7},{7,5},{8,10},{10,8},{9,1... | collective-permute-start | bytes 6152 | tf_op jit(solution)/shard_map/ppermute | solution.py:326
  7.4 24.4 %all-to-all-start.1 = ((bf16[16,24,1024]{2,1,0:T(8,128)(2,1)}), bf16[16,24,1024]{2,1,0:T(8,128)(2,1)S(1)}, u32[]{:S(2)}, u32[]{:S(2)}) async-start(bf16[16,24,1024]{2,1,0:T(8,128)(2,1)} %bitcast.21), calls=%async_computation.1 | async-start | bytes 1572864 | tf_op jit(solution)/shard_map/all_to_all | solution.py:319
  13.4 14.7 %collective-permute-start.2 = (bf16[128,1024]{1,0:T(8,128)(2,1)}, bf16[128,1024]{1,0:T(8,128)(2,1)S(1)}, u32[]{:S(2)}, u32[]{:S(2)}) collective-permute-start(bf16[128,1024]{1,0:T(8,128)(2,1)} %get-tuple-element.11), channel_id=1, source_target_pairs={{0,2},{2,0},{1,3},{3,1},{4,6},{6,4},{5,7},{7,5},{8,10},{10,8},{9,1... | collective-permute-start | bytes 786440 | tf_op jit(solution)/shard_map/ppermute | solution.py:330
  31.8 17.1 %all-to-all-start = ((bf16[16,24,1024]{2,1,0:T(8,128)(2,1)}), bf16[16,24,1024]{2,1,0:T(8,128)(2,1)S(1)}, u32[]{:S(2)}, u32[]{:S(2)}) async-start(bf16[16,24,1024]{2,1,0:T(8,128)(2,1)} %bitcast.2), calls=%async_computation | async-start | bytes 1572864 | tf_op jit(solution)/shard_map/all_to_all | solution.py:319
  48.9 52.8 %copy-start = (f32[256,2]{0,1:T(2,128)S(1)}, f32[256,2]{0,1:T(2,128)}, u32[]{:S(2)}) copy-start(f32[256,2]{0,1:T(2,128)} %param.8) | copy-start | bytes 6148
  48.9 52.8 %copy-start.1 = (s32[2,256]{1,0:T(2,128)S(1)}, s32[2,256]{1,0:T(2,128)}, u32[]{:S(2)}) copy-start(s32[2,256]{1,0:T(2,128)} %get-tuple-element.9.target_ref) | copy-start | bytes 6148

commit v4 on v3

--- a/solution.py
+++ b/solution.py
@@ -10,6 +10,7 @@
 LANES = 128
 SUBLANES = 8
 SMALL = 8 << 20
+PARTS = (2, 2, 4, 4, 4)
 NN = (((1,), (0,)), ((), ()))
 NT = (((1,), (1,)), ((), ()))
 TN = (((0,), (0,)), ((), ()))
@@ -116,25 +117,27 @@
     )(pick, tokens, part)
 
 
-def expert_body(blocks, packed, far, *refs):
+def expert_body(sizes, packed, far, *refs):
     x_hbm, p_hbm, wo_hbm, wi_hbm = refs[:4]
     near_hbm = refs[4] if far else None
-    o_ref, x, p, wo, wi, acc, gsum, sem = refs[4 + far :]
+    o_ref, x, acc, gsum, sem, *bufs = refs[4 + far :]
     rows, width = x.shape
-    size = wo.shape[1]
+    blocks = len(sizes)
+    p, wo, wi = bufs[:blocks], bufs[blocks : 2 * blocks], bufs[2 * blocks :]
     own = lax.axis_index("half")
     half = 1 - own if far else own
 
+    def block(j):
+        return pl.ds(sum(sizes[:j]), sizes[j])
+
     def up(j):
-        return pltpu.make_async_copy(wo_hbm.at[pl.ds(j * size, size), :], wo.at[j], sem.at[0, j])
+        return pltpu.make_async_copy(wo_hbm.at[block(j), :], wo[j], sem.at[0, j])
 
     def pre(j):
-        return pltpu.make_async_copy(
-            p_hbm.at[:, half, :, pl.ds(j * size, size)], p.at[j], sem.at[1, j]
-        )
+        return pltpu.make_async_copy(p_hbm.at[:, half, :, block(j)], p[j], sem.at[1, j])
 
     def down(j):
-        return pltpu.make_async_copy(wi_hbm.at[:, pl.ds(j * size, size)], wi.at[j], sem.at[2, j])
+        return pltpu.make_async_copy(wi_hbm.at[:, block(j)], wi[j], sem.at[2, j])
 
     rows_in = pltpu.make_async_copy(x_hbm, x, sem.at[3, 0])
     rows_in.start()
@@ -147,21 +150,21 @@
         near.start()
     rows_in.wait()
     up(0).wait()
-    upstream = matmul(x[...], wo[0], NT)
+    upstream = matmul(x[...], wo[0][...], NT)
     for j in range(blocks):
         pre(j).wait()
         down(j).wait()
         following = None
         if j + 1 < blocks:
             up(j + 1).wait()
-            following = matmul(x[...], wo[j + 1], NT)
-        act = p[j].astype(jnp.float32).reshape(rows, size)
+            following = matmul(x[...], wo[j + 1][...], NT)
+        act = p[j][...].astype(jnp.float32).reshape(rows, sizes[j])
         prod = jnp.maximum(act, 0.0) * upstream
         part = prod[:, :LANES]
-        for q in range(1, size // LANES):
+        for q in range(1, sizes[j] // LANES):
             part = part + prod[:, q * LANES : (q + 1) * LANES]
         hidden = jnp.where(act > 0, upstream, 0.0).astype(jnp.bfloat16)
-        back = matmul(hidden, wi[j], NT)
+        back = matmul(hidden, wi[j][...], NT)
         if j == 0:
             acc[...] = back
             gsum[...] = part
@@ -203,10 +206,10 @@
     )
 
 
-def expert(x, p, wo, wi, rest, blocks, near=None):
+def expert(x, p, wo, wi, rest, near=None):
     rows, width = x.shape
     outer, _, group, hidden = p.shape
-    size = hidden // blocks
+    sizes = [part * hidden // sum(PARTS) for part in PARTS]
     per_peer = group // rest
     far = near is not None
     packed = per_peer % SUBLANES == 0
@@ -218,22 +221,19 @@
     )
     operands = (x, p, wo, wi) + ((near,) if far else ())
     return pl.pallas_call(
-        functools.partial(expert_body, blocks, packed, int(far)),
+        functools.partial(expert_body, sizes, packed, int(far)),
         out_shape=jax.ShapeDtypeStruct(shape, jnp.bfloat16),
-        in_specs=[
-            pl.BlockSpec(memory_space=pltpu.HBM if 1 <= i <= 3 else pl.ANY)
-            for i in range(len(operands))
-        ],
+        in_specs=[pl.BlockSpec(memory_space=pl.ANY)] * len(operands),
         out_specs=pl.BlockSpec(memory_space=pltpu.VMEM),
         scratch_shapes=[
             pltpu.VMEM((rows, width), jnp.bfloat16),
-            pltpu.VMEM((blocks, outer, group, size), jnp.bfloat16),
-            pltpu.VMEM((blocks, size, width), jnp.bfloat16),
-            pltpu.VMEM((blocks, width, size), jnp.bfloat16),
             pltpu.VMEM((rows, width), jnp.float32),
             pltpu.VMEM((rows, LANES), jnp.float32),
-            pltpu.SemaphoreType.DMA((4, blocks)),
-        ],
+            pltpu.SemaphoreType.DMA((4, len(sizes))),
+        ]
+        + [pltpu.VMEM((outer, group, size), jnp.bfloat16) for size in sizes]
+        + [pltpu.VMEM((size, width), jnp.bfloat16) for size in sizes]
+        + [pltpu.VMEM((width, size), jnp.bfloat16) for size in sizes],
         compiler_params=pltpu.CompilerParams(vmem_limit_bytes=50 << 20),
         cost_estimate=pl.CostEstimate(
             flops=4 * rows * width * hidden,
@@ -258,8 +258,7 @@
     weight = jnp.where(
         hit[0], gate_ref[0:1, :], jnp.where(hit[1], gate_ref[1:2, :], 0.0)
     )
-    high = weight.astype(jnp.bfloat16)
-    low = (weight - high.astype(jnp.float32)).astype(jnp.bfloat16)
+    weight = weight.astype(jnp.bfloat16)
     if packed:
 
         def column(c):
@@ -280,12 +279,12 @@
         )
         for c in range(0, cols, 2):
             part = jnp.concatenate([column(c), column(c + 1)], axis=1)
-            grad_ref[:, c * LANES : (c + 2) * LANES] = (
-                matmul(high, part, TN) + matmul(low, part, TN)
-            ).astype(jnp.bfloat16)
+            grad_ref[:, c * LANES : (c + 2) * LANES] = matmul(weight, part, TN).astype(
+                jnp.bfloat16
+            )
     else:
         part = back_ref[:, :width]
-        grad_ref[...] = (matmul(high, part, TN) + matmul(low, part, TN)).astype(jnp.bfloat16)
+        grad_ref[...] = matmul(weight, part, TN).astype(jnp.bfloat16)
         sums = back_ref[:, width:]
     for k in range(2):
         pick = jnp.where(hit[k], 1.0, 0.0).astype(jnp.bfloat16)
@@ -332,8 +331,8 @@
     part, pick = gather_first(far_ids, first, devices, per_peer, rest)
     far_rows = to_half(gather_last(pick, second, part))
     act = pre_act.reshape(outer, 2, group, hidden)
-    near = expert(near_rows, act, w_out[0], w_in[0], rest, 4)
-    result = expert(far_rows, act, w_out[0], w_in[0], rest, 4, near)
+    near = expert(near_rows, act, w_out[0], w_in[0], rest)
+    result = expert(far_rows, act, w_out[0], w_in[0], rest, near)
     if result.ndim == 5:
         result = result.reshape(devices, *result.shape[3:])
     else:

time: 104 us -> 103 us (level)
  Pallas kernels: 26.2 us -> 25 us
  transfers between devices with their start and end apart: 5 -> 5, of which waited for: 4 -> 4; matrix products, arithmetic and copies ran while one was open for 0% -> 0% of each run, Pallas kernels for 14% -> 13%
where the time goes in v4:
time: 103 us
  blocking collectives  42.8 us (42%)
  Pallas kernels  25 us (24%)
  starting transfers between devices  17.3 us (17%)
  waiting for transfers between devices  16.1 us (16%)
    all_to_all x1, blocking collectives, exchange(): return lax.all_to_all(x, axes, split_axis=0, concat_axis=0, tiled=True)  42.8 us
    pallas_call x2, Pallas kernels, expert(): pl.pallas_call(functools.partial(expert_body, sizes, packed, int(far)), o...  19.2 us
    all_to_all x2, starting transfers between devices, exchange(): return lax.all_to_all(x, axes, split_axis=0, concat_axis=0, tiled=True)  11.7 us
    ppermute x1, waiting for transfers between devices, per_device(): second = lax.ppermute(late, 'half', swap)  10.9 us
    all_to_all x2, waiting for transfers between devices, exchange(): return lax.all_to_all(x, axes, split_axis=0, concat_axis=0, tiled=True)  4.26 us
    ppermute x1, starting transfers between devices, per_device(): first = lax.ppermute(output_grad[:early], 'half', swap)  3.2 us
    pallas_call x1, Pallas kernels, route(): pl.pallas_call(functools.partial(route_body, experts, per_peer, rest), ou...  2.51 us
    ppermute x1, starting transfers between devices, per_device(): second = lax.ppermute(late, 'half', swap)  2.31 us
  transfers between devices with their start and end apart: 5, of which 4 were waited for; matrix products, arithmetic and copies ran while one was open for 0% of the time, Pallas kernels for 13%

profile of v4, /device:TPU:1, one launch (start us, length us, event | category | flops | bytes accessed | tf_op | source)
XLA Modules:
  0.0 102.8 jit_solution(13853674178561050657)
XLA Ops:
  0.6 1.0 slice.3
  1.6 3.2 %collective-permute-start.1 = (bf16[128,1024]{1,0:T(8,128)(2,1)S(1)}, bf16[128,1024]{1,0:T(8,128)(2,1)S(1)}, u32[]{:S(2)}, u32[]{:S(2)}) collective-permute-start(bf16[128,1024]{1,0:T(8,128)(2,1)S(1)} %slice.3), channel_id=1, source_target_pairs={{0,2},{2,0},{1,3},{3,1},{4,6},{6,4},{5,7},{7,5},{8,10},{10,8},{9,1... | collective-permute-start | bytes 786440 | tf_op jit(solution)/shard_map/ppermute | solution.py:327
  4.8 0.1 collective-permute-start
  4.9 2.5 %route.1 = (bf16[384,1024]{1,0:T(8,128)(2,1)}, s32[2,256]{1,0:T(2,128)}, bf16[128,1024]{1,0:T(8,128)(2,1)}) custom-call(s32[2,256]{1,0:T(2,128)} %bitcast.23, bf16[256,1024]{1,0:T(8,128)(2,1)} %tok_ref.1), custom_call_target="tpu_custom_call" | custom-call | flops 201326592 | bytes 1310720 | tf_op jit(solution)/shard_map/route/pallas_call | solution.py:63
  7.4 6.0 %all-to-all-start.1 = ((bf16[16,24,1024]{2,1,0:T(8,128)(2,1)}), bf16[16,24,1024]{2,1,0:T(8,128)(2,1)S(1)}, u32[]{:S(2)}, u32[]{:S(2)}) async-start(bf16[16,24,1024]{2,1,0:T(8,128)(2,1)} %bitcast.21), calls=%async_computation.1 | async-start | bytes 1572864 | tf_op jit(solution)/shard_map/all_to_all | solution.py:318
  13.4 2.3 %collective-permute-start.2 = (bf16[128,1024]{1,0:T(8,128)(2,1)}, bf16[128,1024]{1,0:T(8,128)(2,1)S(1)}, u32[]{:S(2)}, u32[]{:S(2)}) collective-permute-start(bf16[128,1024]{1,0:T(8,128)(2,1)} %get-tuple-element.11), channel_id=1, source_target_pairs={{0,2},{2,0},{1,3},{3,1},{4,6},{6,4},{5,7},{7,5},{8,10},{10,8},{9,1... | collective-permute-start | bytes 786440 | tf_op jit(solution)/shard_map/ppermute | solution.py:329
  15.7 0.9 collective-permute-done.ids_ref
  16.5 0.0 collective-permute-done.1.tok_ref
  16.5 0.5 gather_first.1
  17.1 10.9 %collective-permute-done.2.tok_ref = bf16[128,1024]{1,0:T(8,128)(2,1)S(1)} collective-permute-done((bf16[128,1024]{1,0:T(8,128)(2,1)}, bf16[128,1024]{1,0:T(8,128)(2,1)S(1)}, u32[]{:S(2)}, u32[]{:S(2)}) %collective-permute-start.2) | collective-permute-done | bytes 262176 | tf_op jit(solution)/shard_map/ppermute | solution.py:329
  28.0 1.3 %gather_last.1 = bf16[384,1024]{1,0:T(8,128)(2,1)} custom-call(bf16[384,128]{1,0:T(8,128)(2,1)S(1)} %get-tuple-element.10.pick_ref, bf16[128,1024]{1,0:T(8,128)(2,1)S(1)} %collective-permute-done.2.tok_ref, bf16[384,1024]{1,0:T(8,128)(2,1)S(1)} %get-tuple-element.12.part_ref), custom_call_target="tpu_custom_call" | custom-call | flops 100663296 | tf_op jit(solution)/shard_map/gather_last/pallas_call | solution.py:109
  29.3 2.5 %all-to-all-done.1 = bf16[16,24,1024]{2,1,0:T(8,128)(2,1)S(1)} async-done(((bf16[16,24,1024]{2,1,0:T(8,128)(2,1)}), bf16[16,24,1024]{2,1,0:T(8,128)(2,1)S(1)}, u32[]{:S(2)}, u32[]{:S(2)}) %all-to-all-start.1) | async-done | bytes 786464 | tf_op jit(solution)/shard_map/all_to_all | solution.py:318
  31.8 5.8 %all-to-all-start = ((bf16[16,24,1024]{2,1,0:T(8,128)(2,1)}), bf16[16,24,1024]{2,1,0:T(8,128)(2,1)S(1)}, u32[]{:S(2)}, u32[]{:S(2)}) async-start(bf16[16,24,1024]{2,1,0:T(8,128)(2,1)} %bitcast.2), calls=%async_computation | async-start | bytes 1572864 | tf_op jit(solution)/shard_map/all_to_all | solution.py:318
  37.6 9.5 %expert_near.1.refs_4_ = bf16[8,2,200,128]{3,2,1,0:T(8,128)(2,1)S(1)} custom-call(bf16[384,1024]{1,0:T(8,128)(2,1)S(1)} %bitcast.12, bf16[8,2,48,4096]{3,2,1,0:T(8,128)(2,1)} %bitcast.19, bf16[4096,1024]{1,0:T(8,128)(2,1)} %bitcast.15, bf16[1024,4096]{1,0:T(8,128)(2,1)} %bitcast.17), custom_call_target="tpu_custom_call" | custom-call | flops 6442450944 | bytes 21495808 | tf_op jit(solution)/shard_map/expert_near/pallas_call | solution.py:223
  47.1 1.8 %all-to-all-done = bf16[16,24,1024]{2,1,0:T(8,128)(2,1)S(1)} async-done(((bf16[16,24,1024]{2,1,0:T(8,128)(2,1)}), bf16[16,24,1024]{2,1,0:T(8,128)(2,1)S(1)}, u32[]{:S(2)}, u32[]{:S(2)}) %all-to-all-start) | async-done | bytes 786464 | tf_op jit(solution)/shard_map/all_to_all | solution.py:318
  48.9 0.0 copy-start
  48.9 0.0 copy-start.1
  48.9 9.7 %expert_far.1 = bf16[8,2,2,200,128]{4,3,2,1,0:T(8,128)(2,1)S(1)} custom-call(bf16[384,1024]{1,0:T(8,128)(2,1)S(1)} %bitcast.13, bf16[8,2,48,4096]{3,2,1,0:T(8,128)(2,1)} %bitcast.20, bf16[4096,1024]{1,0:T(8,128)(2,1)} %bitcast.16, bf16[1024,4096]{1,0:T(8,128)(2,1)} %bitcast.18, bf16[8,2,200,128]{3,2,1,0:T(8,128)(2,1)S(1)} %expert_near.1.refs_4_), custom_call_target="tpu_custom_call" | custom-call | flops 6442450944 | bytes 21495808 | tf_op jit(solution)/shard_map/expert_far/pallas_call | solution.py:223
  58.5 42.8 %all_to_all.15.back_ref = bf16[32,200,128]{2,1,0:T(8,128)(2,1)S(1)} all-to-all(bf16[32,200,128]{2,1,0:T(8,128)(2,1)S(1)} %bitcast.11), channel_id=1, replica_groups=mesh['outer'=8,'half'=2,'rest'=2] {'outer','half','rest'}, dimensions={0} | all-to-all | bytes 3276800 | tf_op jit(solution)/shard_map/all_to_all | solution.py:318
  101.3 0.0 copy-done
  101.3 0.0 copy-done.1
  101.3 1.5 %combine.1 = (bf16[256,1024]{1,0:T(8,128)(2,1)}, f32[2,256]{1,0:T(2,128)}) custom-call(s32[2,256]{1,0:T(2,128)S(1)} %copy-done.1, f32[2,256]{1,0:T(2,128)S(1)} %bitcast.14, bf16[32,200,128]{2,1,0:T(8,128)(2,1)S(1)} %all_to_all.15.back_ref), custom_call_target="tpu_custom_call" | custom-call | tf_op jit(solution)/shard_map/combine/pallas_call | solution.py:297
Async XLA Ops:
  1.6 14.9 %collective-permute-start.1 = (bf16[128,1024]{1,0:T(8,128)(2,1)S(1)}, bf16[128,1024]{1,0:T(8,128)(2,1)S(1)}, u32[]{:S(2)}, u32[]{:S(2)}) collective-permute-start(bf16[128,1024]{1,0:T(8,128)(2,1)S(1)} %slice.3), channel_id=1, source_target_pairs={{0,2},{2,0},{1,3},{3,1},{4,6},{6,4},{5,7},{7,5},{8,10},{10,8},{9,1... | collective-permute-start | bytes 786440 | tf_op jit(solution)/shard_map/ppermute | solution.py:327
  4.8 11.7 %collective-permute-start = (s32[2,256]{1,0:T(2,128)}, s32[2,256]{1,0:T(2,128)S(1)}, u32[]{:S(2)}, u32[]{:S(2)}) collective-permute-start(s32[2,256]{1,0:T(2,128)} %bitcast.22), channel_id=1, source_target_pairs={{0,2},{2,0},{1,3},{3,1},{4,6},{6,4},{5,7},{7,5},{8,10},{10,8},{9,1... | collective-permute-start | bytes 6152 | tf_op jit(solution)/shard_map/ppermute | solution.py:325
  7.4 24.4 %all-to-all-start.1 = ((bf16[16,24,1024]{2,1,0:T(8,128)(2,1)}), bf16[16,24,1024]{2,1,0:T(8,128)(2,1)S(1)}, u32[]{:S(2)}, u32[]{:S(2)}) async-start(bf16[16,24,1024]{2,1,0:T(8,128)(2,1)} %bitcast.21), calls=%async_computation.1 | async-start | bytes 1572864 | tf_op jit(solution)/shard_map/all_to_all | solution.py:318
  13.4 14.7 %collective-permute-start.2 = (bf16[128,1024]{1,0:T(8,128)(2,1)}, bf16[128,1024]{1,0:T(8,128)(2,1)S(1)}, u32[]{:S(2)}, u32[]{:S(2)}) collective-permute-start(bf16[128,1024]{1,0:T(8,128)(2,1)} %get-tuple-element.11), channel_id=1, source_target_pairs={{0,2},{2,0},{1,3},{3,1},{4,6},{6,4},{5,7},{7,5},{8,10},{10,8},{9,1... | collective-permute-start | bytes 786440 | tf_op jit(solution)/shard_map/ppermute | solution.py:329
  31.8 17.1 %all-to-all-start = ((bf16[16,24,1024]{2,1,0:T(8,128)(2,1)}), bf16[16,24,1024]{2,1,0:T(8,128)(2,1)S(1)}, u32[]{:S(2)}, u32[]{:S(2)}) async-start(bf16[16,24,1024]{2,1,0:T(8,128)(2,1)} %bitcast.2), calls=%async_computation | async-start | bytes 1572864 | tf_op jit(solution)/shard_map/all_to_all | solution.py:318
  48.9 52.4 %copy-start = (f32[256,2]{0,1:T(2,128)S(1)}, f32[256,2]{0,1:T(2,128)}, u32[]{:S(2)}) copy-start(f32[256,2]{0,1:T(2,128)} %param.8) | copy-start | bytes 6148
  48.9 52.4 %copy-start.1 = (s32[2,256]{1,0:T(2,128)S(1)}, s32[2,256]{1,0:T(2,128)}, u32[]{:S(2)}) copy-start(s32[2,256]{1,0:T(2,128)} %get-tuple-element.9.target_ref) | copy-start | bytes 6148

commit v5 on v4

--- a/solution.py
+++ b/solution.py
@@ -323,7 +323,7 @@
 
     ids = expert_ids.T
     far_ids = lax.ppermute(ids, "half", swap)
-    early = output_grad.shape[0] // 2
+    early = output_grad.shape[0] * 15 // 32
     first = lax.ppermute(output_grad[:early], "half", swap)
     send, target, late = route(ids, output_grad, early, devices, per_peer, rest)
     second = lax.ppermute(late, "half", swap)

time: 103 us -> 103 us (level)
    ppermute x1, waiting for transfers between devices: 10.9 us -> 12 us  [per_device(): second = lax.ppermute(late, 'half', swap)]
  transfers between devices with their start and end apart: 5 -> 5, of which waited for: 4 -> 4; matrix products, arithmetic and copies ran while one was open for 0% -> 0% of each run, Pallas kernels for 13% -> 14%
where the time goes in v5:
time: 103 us; the launch traced here: 102 us
  blocking collectives  42 us (41%)
  Pallas kernels  25 us (24%)
  starting transfers between devices  18.1 us (18%)
  waiting for transfers between devices  15.7 us (15%)
    all_to_all x1, blocking collectives, exchange(): return lax.all_to_all(x, axes, split_axis=0, concat_axis=0, tiled=True)  42 us
    pallas_call x2, Pallas kernels, expert(): pl.pallas_call(functools.partial(expert_body, sizes, packed, int(far)), o...  19.2 us
    all_to_all x2, starting transfers between devices, exchange(): return lax.all_to_all(x, axes, split_axis=0, concat_axis=0, tiled=True)  12.5 us
    ppermute x1, waiting for transfers between devices, per_device(): second = lax.ppermute(late, 'half', swap)  12 us
    all_to_all x2, waiting for transfers between devices, exchange(): return lax.all_to_all(x, axes, split_axis=0, concat_axis=0, tiled=True)  3.45 us
    ppermute x1, starting transfers between devices, per_device(): first = lax.ppermute(output_grad[:early], 'half', swap)  3.2 us
    pallas_call x1, Pallas kernels, route(): pl.pallas_call(functools.partial(route_body, experts, per_peer, rest), ou...  2.52 us
    ppermute x1, starting transfers between devices, per_device(): second = lax.ppermute(late, 'half', swap)  2.31 us
  transfers between devices with their start and end apart: 5, of which 4 were waited for; matrix products, arithmetic and copies ran while one was open for 0% of the time, Pallas kernels for 14%

profile of v5, /device:TPU:1, one launch (start us, length us, event | category | flops | bytes accessed | tf_op | source)
XLA Modules:
  0.0 102.5 jit_solution(3835280938183799937)
XLA Ops:
  0.6 1.0 slice.3
  1.6 3.2 %collective-permute-start.1 = (bf16[120,1024]{1,0:T(8,128)(2,1)S(1)}, bf16[120,1024]{1,0:T(8,128)(2,1)S(1)}, u32[]{:S(2)}, u32[]{:S(2)}) collective-permute-start(bf16[120,1024]{1,0:T(8,128)(2,1)S(1)} %slice.3), channel_id=1, source_target_pairs={{0,2},{2,0},{1,3},{3,1},{4,6},{6,4},{5,7},{7,5},{8,10},{10,8},{9,1... | collective-permute-start | bytes 737288 | tf_op jit(solution)/shard_map/ppermute | solution.py:327
  4.8 0.1 collective-permute-start
  4.9 2.5 %route.1 = (bf16[384,1024]{1,0:T(8,128)(2,1)}, s32[2,256]{1,0:T(2,128)}, bf16[136,1024]{1,0:T(8,128)(2,1)}) custom-call(s32[2,256]{1,0:T(2,128)} %bitcast.23, bf16[256,1024]{1,0:T(8,128)(2,1)} %tok_ref.1), custom_call_target="tpu_custom_call" | custom-call | flops 201326592 | bytes 1310720 | tf_op jit(solution)/shard_map/route/pallas_call | solution.py:63
  7.4 6.0 %all-to-all-start.1 = ((bf16[16,24,1024]{2,1,0:T(8,128)(2,1)}), bf16[16,24,1024]{2,1,0:T(8,128)(2,1)S(1)}, u32[]{:S(2)}, u32[]{:S(2)}) async-start(bf16[16,24,1024]{2,1,0:T(8,128)(2,1)} %bitcast.21), calls=%async_computation.1 | async-start | bytes 1572864 | tf_op jit(solution)/shard_map/all_to_all | solution.py:318
  13.4 2.3 %collective-permute-start.2 = (bf16[136,1024]{1,0:T(8,128)(2,1)}, bf16[136,1024]{1,0:T(8,128)(2,1)S(1)}, u32[]{:S(2)}, u32[]{:S(2)}) collective-permute-start(bf16[136,1024]{1,0:T(8,128)(2,1)} %get-tuple-element.11), channel_id=1, source_target_pairs={{0,2},{2,0},{1,3},{3,1},{4,6},{6,4},{5,7},{7,5},{8,10},{10,8},{9,1... | collective-permute-start | bytes 835592 | tf_op jit(solution)/shard_map/ppermute | solution.py:329
  15.7 0.2 collective-permute-done.ids_ref
  15.8 0.0 collective-permute-done.1.tok_ref
  15.8 0.5 gather_first.1
  16.4 12.0 %collective-permute-done.2.tok_ref = bf16[136,1024]{1,0:T(8,128)(2,1)S(1)} collective-permute-done((bf16[136,1024]{1,0:T(8,128)(2,1)}, bf16[136,1024]{1,0:T(8,128)(2,1)S(1)}, u32[]{:S(2)}, u32[]{:S(2)}) %collective-permute-start.2) | collective-permute-done | bytes 278560 | tf_op jit(solution)/shard_map/ppermute | solution.py:329
  28.4 1.3 %gather_last.1 = bf16[384,1024]{1,0:T(8,128)(2,1)} custom-call(bf16[384,136]{1,0:T(8,128)(2,1)S(1)} %get-tuple-element.10.pick_ref, bf16[136,1024]{1,0:T(8,128)(2,1)S(1)} %collective-permute-done.2.tok_ref, bf16[384,1024]{1,0:T(8,128)(2,1)S(1)} %get-tuple-element.12.part_ref), custom_call_target="tpu_custom_call" | custom-call | flops 106954752 | tf_op jit(solution)/shard_map/gather_last/pallas_call | solution.py:109
  29.7 1.7 %all-to-all-done.1 = bf16[16,24,1024]{2,1,0:T(8,128)(2,1)S(1)} async-done(((bf16[16,24,1024]{2,1,0:T(8,128)(2,1)}), bf16[16,24,1024]{2,1,0:T(8,128)(2,1)S(1)}, u32[]{:S(2)}, u32[]{:S(2)}) %all-to-all-start.1) | async-done | bytes 786464 | tf_op jit(solution)/shard_map/all_to_all | solution.py:318
  31.4 6.5 %all-to-all-start = ((bf16[16,24,1024]{2,1,0:T(8,128)(2,1)}), bf16[16,24,1024]{2,1,0:T(8,128)(2,1)S(1)}, u32[]{:S(2)}, u32[]{:S(2)}) async-start(bf16[16,24,1024]{2,1,0:T(8,128)(2,1)} %bitcast.2), calls=%async_computation | async-start | bytes 1572864 | tf_op jit(solution)/shard_map/all_to_all | solution.py:318
  37.9 9.5 %expert_near.1.refs_4_ = bf16[8,2,200,128]{3,2,1,0:T(8,128)(2,1)S(1)} custom-call(bf16[384,1024]{1,0:T(8,128)(2,1)S(1)} %bitcast.12, bf16[8,2,48,4096]{3,2,1,0:T(8,128)(2,1)} %bitcast.19, bf16[4096,1024]{1,0:T(8,128)(2,1)} %bitcast.15, bf16[1024,4096]{1,0:T(8,128)(2,1)} %bitcast.17), custom_call_target="tpu_custom_call" | custom-call | flops 6442450944 | bytes 21495808 | tf_op jit(solution)/shard_map/expert_near/pallas_call | solution.py:223
  47.5 1.7 %all-to-all-done = bf16[16,24,1024]{2,1,0:T(8,128)(2,1)S(1)} async-done(((bf16[16,24,1024]{2,1,0:T(8,128)(2,1)}), bf16[16,24,1024]{2,1,0:T(8,128)(2,1)S(1)}, u32[]{:S(2)}, u32[]{:S(2)}) %all-to-all-start) | async-done | bytes 786464 | tf_op jit(solution)/shard_map/all_to_all | solution.py:318
  49.2 0.0 copy-start
  49.2 0.0 copy-start.1
  49.2 9.7 %expert_far.1 = bf16[8,2,2,200,128]{4,3,2,1,0:T(8,128)(2,1)S(1)} custom-call(bf16[384,1024]{1,0:T(8,128)(2,1)S(1)} %bitcast.13, bf16[8,2,48,4096]{3,2,1,0:T(8,128)(2,1)} %bitcast.20, bf16[4096,1024]{1,0:T(8,128)(2,1)} %bitcast.16, bf16[1024,4096]{1,0:T(8,128)(2,1)} %bitcast.18, bf16[8,2,200,128]{3,2,1,0:T(8,128)(2,1)S(1)} %expert_near.1.refs_4_), custom_call_target="tpu_custom_call" | custom-call | flops 6442450944 | bytes 21495808 | tf_op jit(solution)/shard_map/expert_far/pallas_call | solution.py:223
  58.9 42.0 %all_to_all.15.back_ref = bf16[32,200,128]{2,1,0:T(8,128)(2,1)S(1)} all-to-all(bf16[32,200,128]{2,1,0:T(8,128)(2,1)S(1)} %bitcast.11), channel_id=1, replica_groups=mesh['outer'=8,'half'=2,'rest'=2] {'outer','half','rest'}, dimensions={0} | all-to-all | bytes 3276800 | tf_op jit(solution)/shard_map/all_to_all | solution.py:318
  100.9 0.0 copy-done
  100.9 0.0 copy-done.1
  100.9 1.5 %combine.1 = (bf16[256,1024]{1,0:T(8,128)(2,1)}, f32[2,256]{1,0:T(2,128)}) custom-call(s32[2,256]{1,0:T(2,128)S(1)} %copy-done.1, f32[2,256]{1,0:T(2,128)S(1)} %bitcast.14, bf16[32,200,128]{2,1,0:T(8,128)(2,1)S(1)} %all_to_all.15.back_ref), custom_call_target="tpu_custom_call" | custom-call | tf_op jit(solution)/shard_map/combine/pallas_call | solution.py:297
Async XLA Ops:
  1.6 14.2 %collective-permute-start.1 = (bf16[120,1024]{1,0:T(8,128)(2,1)S(1)}, bf16[120,1024]{1,0:T(8,128)(2,1)S(1)}, u32[]{:S(2)}, u32[]{:S(2)}) collective-permute-start(bf16[120,1024]{1,0:T(8,128)(2,1)S(1)} %slice.3), channel_id=1, source_target_pairs={{0,2},{2,0},{1,3},{3,1},{4,6},{6,4},{5,7},{7,5},{8,10},{10,8},{9,1... | collective-permute-start | bytes 737288 | tf_op jit(solution)/shard_map/ppermute | solution.py:327
  4.8 11.0 %collective-permute-start = (s32[2,256]{1,0:T(2,128)}, s32[2,256]{1,0:T(2,128)S(1)}, u32[]{:S(2)}, u32[]{:S(2)}) collective-permute-start(s32[2,256]{1,0:T(2,128)} %bitcast.22), channel_id=1, source_target_pairs={{0,2},{2,0},{1,3},{3,1},{4,6},{6,4},{5,7},{7,5},{8,10},{10,8},{9,1... | collective-permute-start | bytes 6152 | tf_op jit(solution)/shard_map/ppermute | solution.py:325
  7.4 24.0 %all-to-all-start.1 = ((bf16[16,24,1024]{2,1,0:T(8,128)(2,1)}), bf16[16,24,1024]{2,1,0:T(8,128)(2,1)S(1)}, u32[]{:S(2)}, u32[]{:S(2)}) async-start(bf16[16,24,1024]{2,1,0:T(8,128)(2,1)} %bitcast.21), calls=%async_computation.1 | async-start | bytes 1572864 | tf_op jit(solution)/shard_map/all_to_all | solution.py:318
  13.4 15.1 %collective-permute-start.2 = (bf16[136,1024]{1,0:T(8,128)(2,1)}, bf16[136,1024]{1,0:T(8,128)(2,1)S(1)}, u32[]{:S(2)}, u32[]{:S(2)}) collective-permute-start(bf16[136,1024]{1,0:T(8,128)(2,1)} %get-tuple-element.11), channel_id=1, source_target_pairs={{0,2},{2,0},{1,3},{3,1},{4,6},{6,4},{5,7},{7,5},{8,10},{10,8},{9,1... | collective-permute-start | bytes 835592 | tf_op jit(solution)/shard_map/ppermute | solution.py:329
  31.4 17.8 %all-to-all-start = ((bf16[16,24,1024]{2,1,0:T(8,128)(2,1)}), bf16[16,24,1024]{2,1,0:T(8,128)(2,1)S(1)}, u32[]{:S(2)}, u32[]{:S(2)}) async-start(bf16[16,24,1024]{2,1,0:T(8,128)(2,1)} %bitcast.2), calls=%async_computation | async-start | bytes 1572864 | tf_op jit(solution)/shard_map/all_to_all | solution.py:318
  49.2 51.7 %copy-start = (f32[256,2]{0,1:T(2,128)S(1)}, f32[256,2]{0,1:T(2,128)}, u32[]{:S(2)}) copy-start(f32[256,2]{0,1:T(2,128)} %param.8) | copy-start | bytes 6148
  49.2 51.7 %copy-start.1 = (s32[2,256]{1,0:T(2,128)S(1)}, s32[2,256]{1,0:T(2,128)}, u32[]{:S(2)}) copy-start(s32[2,256]{1,0:T(2,128)} %get-tuple-element.9.target_ref) | copy-start | bytes 6148

commit v6 on v5

--- a/solution.py
+++ b/solution.py
@@ -77,7 +77,13 @@
     )(ids, tokens)
 
 
-def gather_first_body(experts, per_peer, rest, ids_ref, tok_ref, part_ref, pick_ref):
+def gather_first_body(
+    experts, per_peer, rest, ids_ref, tok_ref, target_ref, gate_ref, part_ref, pick_ref, weight_ref
+):
+    row = lax.broadcasted_iota(jnp.int32, weight_ref.shape[::-1], 0)
+    weight = jnp.where(row == target_ref[1:2, :], gate_ref[1:2, :], 0.0)
+    weight = jnp.where(row == target_ref[0:1, :], gate_ref[0:1, :], weight)
+    weight_ref[...] = weight.T.astype(jnp.bfloat16)
     ids = ids_ref[...]
     pick = pick_rows(ids, slots(ids, experts), part_ref.shape[0], per_peer, rest)
     count = tok_ref.shape[0]
@@ -85,18 +91,19 @@
     pick_ref[...] = pick[:, count:]
 
 
-def gather_first(ids, tokens, experts, per_peer, rest):
+def gather_first(ids, tokens, target, gates, experts, per_peer, rest):
     rows, width = experts // 2 * per_peer, tokens.shape[1]
     return pl.pallas_call(
         functools.partial(gather_first_body, experts, per_peer, rest),
         out_shape=(
             jax.ShapeDtypeStruct((rows, width), jnp.bfloat16),
             jax.ShapeDtypeStruct((rows, ids.shape[1] - tokens.shape[0]), jnp.bfloat16),
+            jax.ShapeDtypeStruct((ids.shape[1], experts * per_peer), jnp.bfloat16),
         ),
         compiler_params=pltpu.CompilerParams(vmem_limit_bytes=SMALL),
         cost_estimate=pl.CostEstimate(flops=40 * 10**9, bytes_accessed=0, transcendentals=0),
         name="gather_first",
-    )(ids, tokens)
+    )(ids, tokens, target, gates)
 
 
 def gather_last_body(pick_ref, tok_ref, part_ref, send_ref):
@@ -244,7 +251,7 @@
     )(*operands)
 
 
-def combine_body(packed, target_ref, gate_ref, back_ref, grad_ref, dots_ref):
+def combine_body(packed, target_ref, weight_ref, back_ref, grad_ref, dots_ref):
     tokens, width = grad_ref.shape
     if packed:
         peers = back_ref.shape[0]
@@ -255,10 +262,7 @@
         rows = back_ref.shape[0]
     row = lax.broadcasted_iota(jnp.int32, (rows, tokens), 0)
     hit = [row == target_ref[k : k + 1, :] for k in range(2)]
-    weight = jnp.where(
-        hit[0], gate_ref[0:1, :], jnp.where(hit[1], gate_ref[1:2, :], 0.0)
-    )
-    weight = weight.astype(jnp.bfloat16)
+    weight = weight_ref[...]
     if packed:
 
         def column(c):
@@ -279,30 +283,30 @@
         )
         for c in range(0, cols, 2):
             part = jnp.concatenate([column(c), column(c + 1)], axis=1)
-            grad_ref[:, c * LANES : (c + 2) * LANES] = matmul(weight, part, TN).astype(
+            grad_ref[:, c * LANES : (c + 2) * LANES] = matmul(weight, part, NN).astype(
                 jnp.bfloat16
             )
     else:
         part = back_ref[:, :width]
-        grad_ref[...] = matmul(weight, part, TN).astype(jnp.bfloat16)
+        grad_ref[...] = matmul(weight, part, NN).astype(jnp.bfloat16)
         sums = back_ref[:, width:]
     for k in range(2):
         pick = jnp.where(hit[k], 1.0, 0.0).astype(jnp.bfloat16)
         dots_ref[k : k + 1, :] = jnp.sum(matmul(sums, pick, TN), axis=0, keepdims=True)
 
 
-def combine(target, gates, back, width):
-    tokens = gates.shape[1]
+def combine(target, weight, back, width):
+    tokens = target.shape[1]
     packed = back.ndim == 3
     return pl.pallas_call(
         functools.partial(combine_body, packed),
         out_shape=(
             jax.ShapeDtypeStruct((tokens, width), jnp.bfloat16),
-            jax.ShapeDtypeStruct(gates.shape, jnp.float32),
+            jax.ShapeDtypeStruct(target.shape, jnp.float32),
         ),
         compiler_params=pltpu.CompilerParams(vmem_limit_bytes=16 << 20),
         name="combine",
-    )(target, gates, back)
+    )(target, weight, back)
 
 
 def per_device(output_grad, expert_ids, gate_weights, pre_act, w_in, w_out):
@@ -328,7 +332,8 @@
     send, target, late = route(ids, output_grad, early, devices, per_peer, rest)
     second = lax.ppermute(late, "half", swap)
     near_rows = to_half(send)
-    part, pick = gather_first(far_ids, first, devices, per_peer, rest)
+    gates = gate_weights.T
+    part, pick, weight = gather_first(far_ids, first, target, gates, devices, per_peer, rest)
     far_rows = to_half(gather_last(pick, second, part))
     act = pre_act.reshape(outer, 2, group, hidden)
     near = expert(near_rows, act, w_out[0], w_in[0], rest)
@@ -340,7 +345,7 @@
     back = exchange(result, ("outer", "half", "rest"))
     if per_peer % SUBLANES:
         back = back.reshape(cap_rows, -1)
-    input_grad, gate_grad = combine(target, gate_weights.T, back, width)
+    input_grad, gate_grad = combine(target, weight, back, width)
     return input_grad, gate_grad.T
 
 

time: 103 us -> 103 us (level)
  waiting for transfers between devices: 15.7 us -> 14.3 us
  local copies, waits for them, and re-layouts: 0.97 us -> 2.33 us
    ppermute x1, waiting for transfers between devices: 12 us -> 10.6 us  [per_device(): second = lax.ppermute(late, 'half', swap)]
    unnamed x4 -> x6, local copies, waits for them, and re-layouts: 0.01 us -> 1.37 us
where the time goes in v6:
time: 103 us; the launch traced here: 102 us
  blocking collectives  42 us (41%)
  Pallas kernels  24.9 us (24%)
  starting transfers between devices  18.1 us (18%)
  waiting for transfers between devices  14.3 us (14%)
  local copies, waits for them, and re-layouts  2.33 us (2%)
    all_to_all x1, blocking collectives, exchange(): return lax.all_to_all(x, axes, split_axis=0, concat_axis=0, tiled=True)  42 us
    pallas_call x2, Pallas kernels, expert(): pl.pallas_call(functools.partial(expert_body, sizes, packed, int(far)), o...  19.2 us
    all_to_all x2, starting transfers between devices, exchange(): return lax.all_to_all(x, axes, split_axis=0, concat_axis=0, tiled=True)  12.5 us
    ppermute x1, waiting for transfers between devices, per_device(): second = lax.ppermute(late, 'half', swap)  10.6 us
    all_to_all x2, waiting for transfers between devices, exchange(): return lax.all_to_all(x, axes, split_axis=0, concat_axis=0, tiled=True)  3.49 us
    ppermute x1, starting transfers between devices, per_device(): first = lax.ppermute(output_grad[:early], 'half', swap)  3.2 us
    pallas_call x1, Pallas kernels, route(): pl.pallas_call(functools.partial(route_body, experts, per_peer, rest), ou...  2.51 us
    ppermute x1, starting transfers between devices, per_device(): second = lax.ppermute(late, 'half', swap)  2.31 us
  transfers between devices with their start and end apart: 5, of which 4 were waited for; matrix products, arithmetic and copies ran while one was open for 0% of the time, Pallas kernels for 14%

profile of v6, /device:TPU:1, one launch (start us, length us, event | category | flops | bytes accessed | tf_op | source)
XLA Modules:
  0.0 102.3 jit_solution(7597756268308190607)
XLA Ops:
  0.6 1.0 slice.3
  1.6 3.2 %collective-permute-start.1 = (bf16[120,1024]{1,0:T(8,128)(2,1)S(1)}, bf16[120,1024]{1,0:T(8,128)(2,1)S(1)}, u32[]{:S(2)}, u32[]{:S(2)}) collective-permute-start(bf16[120,1024]{1,0:T(8,128)(2,1)S(1)} %slice.3), channel_id=1, source_target_pairs={{0,2},{2,0},{1,3},{3,1},{4,6},{6,4},{5,7},{7,5},{8,10},{10,8},{9,1... | collective-permute-start | bytes 737288 | tf_op jit(solution)/shard_map/ppermute | solution.py:331
  4.8 0.1 collective-permute-start
  4.9 2.5 %route.1 = (bf16[384,1024]{1,0:T(8,128)(2,1)}, s32[2,256]{1,0:T(2,128)}, bf16[136,1024]{1,0:T(8,128)(2,1)}) custom-call(s32[2,256]{1,0:T(2,128)} %bitcast.23, bf16[256,1024]{1,0:T(8,128)(2,1)} %tok_ref.1), custom_call_target="tpu_custom_call" | custom-call | flops 201326592 | bytes 1310720 | tf_op jit(solution)/shard_map/route/pallas_call | solution.py:63
  7.4 6.0 %all-to-all-start.1 = ((bf16[16,24,1024]{2,1,0:T(8,128)(2,1)}), bf16[16,24,1024]{2,1,0:T(8,128)(2,1)S(1)}, u32[]{:S(2)}, u32[]{:S(2)}) async-start(bf16[16,24,1024]{2,1,0:T(8,128)(2,1)} %bitcast.21), calls=%async_computation.1 | async-start | bytes 1572864 | tf_op jit(solution)/shard_map/all_to_all | solution.py:322
  13.4 2.3 %collective-permute-start.2 = (bf16[136,1024]{1,0:T(8,128)(2,1)}, bf16[136,1024]{1,0:T(8,128)(2,1)S(1)}, u32[]{:S(2)}, u32[]{:S(2)}) collective-permute-start(bf16[136,1024]{1,0:T(8,128)(2,1)} %get-tuple-element.13), channel_id=1, source_target_pairs={{0,2},{2,0},{1,3},{3,1},{4,6},{6,4},{5,7},{7,5},{8,10},{10,8},{9,1... | collective-permute-start | bytes 835592 | tf_op jit(solution)/shard_map/ppermute | solution.py:333
  15.7 0.2 collective-permute-done.ids_ref
  15.8 0.0 collective-permute-done.1.tok_ref
  15.8 0.0 copy-start
  15.8 0.7 copy-done
  16.5 0.0 copy-start.2
  16.5 0.7 copy-done.2
  17.2 0.6 gather_first.1
  17.8 10.6 %collective-permute-done.2.tok_ref = bf16[136,1024]{1,0:T(8,128)(2,1)S(1)} collective-permute-done((bf16[136,1024]{1,0:T(8,128)(2,1)}, bf16[136,1024]{1,0:T(8,128)(2,1)S(1)}, u32[]{:S(2)}, u32[]{:S(2)}) %collective-permute-start.2) | collective-permute-done | bytes 278560 | tf_op jit(solution)/shard_map/ppermute | solution.py:333
  28.4 1.3 %gather_last.1 = bf16[384,1024]{1,0:T(8,128)(2,1)} custom-call(bf16[384,136]{1,0:T(8,128)(2,1)S(1)} %get-tuple-element.12.pick_ref, bf16[136,1024]{1,0:T(8,128)(2,1)S(1)} %collective-permute-done.2.tok_ref, bf16[384,1024]{1,0:T(8,128)(2,1)S(1)} %get-tuple-element.14.part_ref), custom_call_target="tpu_custom_call" | custom-call | flops 106954752 | tf_op jit(solution)/shard_map/gather_last/pallas_call | solution.py:116
  29.7 1.7 %all-to-all-done.1 = bf16[16,24,1024]{2,1,0:T(8,128)(2,1)S(1)} async-done(((bf16[16,24,1024]{2,1,0:T(8,128)(2,1)}), bf16[16,24,1024]{2,1,0:T(8,128)(2,1)S(1)}, u32[]{:S(2)}, u32[]{:S(2)}) %all-to-all-start.1) | async-done | bytes 786464 | tf_op jit(solution)/shard_map/all_to_all | solution.py:322
  31.4 6.5 %all-to-all-start = ((bf16[16,24,1024]{2,1,0:T(8,128)(2,1)}), bf16[16,24,1024]{2,1,0:T(8,128)(2,1)S(1)}, u32[]{:S(2)}, u32[]{:S(2)}) async-start(bf16[16,24,1024]{2,1,0:T(8,128)(2,1)} %bitcast.2), calls=%async_computation | async-start | bytes 1572864 | tf_op jit(solution)/shard_map/all_to_all | solution.py:322
  37.9 9.5 %expert_near.1.refs_4_ = bf16[8,2,200,128]{3,2,1,0:T(8,128)(2,1)S(1)} custom-call(bf16[384,1024]{1,0:T(8,128)(2,1)S(1)} %bitcast.12, bf16[8,2,48,4096]{3,2,1,0:T(8,128)(2,1)} %bitcast.19, bf16[4096,1024]{1,0:T(8,128)(2,1)} %bitcast.15, bf16[1024,4096]{1,0:T(8,128)(2,1)} %bitcast.17), custom_call_target="tpu_custom_call" | custom-call | flops 6442450944 | bytes 21495808 | tf_op jit(solution)/shard_map/expert_near/pallas_call | solution.py:230
  47.5 1.7 %all-to-all-done = bf16[16,24,1024]{2,1,0:T(8,128)(2,1)S(1)} async-done(((bf16[16,24,1024]{2,1,0:T(8,128)(2,1)}), bf16[16,24,1024]{2,1,0:T(8,128)(2,1)S(1)}, u32[]{:S(2)}, u32[]{:S(2)}) %all-to-all-start) | async-done | bytes 786464 | tf_op jit(solution)/shard_map/all_to_all | solution.py:322
  49.2 0.0 copy-start.1
  49.2 9.7 %expert_far.1 = bf16[8,2,2,200,128]{4,3,2,1,0:T(8,128)(2,1)S(1)} custom-call(bf16[384,1024]{1,0:T(8,128)(2,1)S(1)} %bitcast.13, bf16[8,2,48,4096]{3,2,1,0:T(8,128)(2,1)} %bitcast.20, bf16[4096,1024]{1,0:T(8,128)(2,1)} %bitcast.16, bf16[1024,4096]{1,0:T(8,128)(2,1)} %bitcast.18, bf16[8,2,200,128]{3,2,1,0:T(8,128)(2,1)S(1)} %expert_near.1.refs_4_), custom_call_target="tpu_custom_call" | custom-call | flops 6442450944 | bytes 21495808 | tf_op jit(solution)/shard_map/expert_far/pallas_call | solution.py:230
  58.9 42.0 %all_to_all.15.back_ref = bf16[32,200,128]{2,1,0:T(8,128)(2,1)S(1)} all-to-all(bf16[32,200,128]{2,1,0:T(8,128)(2,1)S(1)} %bitcast.11), channel_id=1, replica_groups=mesh['outer'=8,'half'=2,'rest'=2] {'outer','half','rest'}, dimensions={0} | all-to-all | bytes 3276800 | tf_op jit(solution)/shard_map/all_to_all | solution.py:322
  100.9 0.0 copy-done.1
  100.9 1.4 %combine.1 = (bf16[256,1024]{1,0:T(8,128)(2,1)}, f32[2,256]{1,0:T(2,128)}) custom-call(s32[2,256]{1,0:T(2,128)S(1)} %copy-done.1, bf16[256,768]{1,0:T(8,128)(2,1)S(1)} %get-tuple-element.11.weight_ref, bf16[32,200,128]{2,1,0:T(8,128)(2,1)S(1)} %all_to_all.15.back_ref), custom_call_target="tpu_custom_call" | custom-call | tf_op jit(solution)/shard_map/combine/pallas_call | solution.py:301
Async XLA Ops:
  1.6 14.2 %collective-permute-start.1 = (bf16[120,1024]{1,0:T(8,128)(2,1)S(1)}, bf16[120,1024]{1,0:T(8,128)(2,1)S(1)}, u32[]{:S(2)}, u32[]{:S(2)}) collective-permute-start(bf16[120,1024]{1,0:T(8,128)(2,1)S(1)} %slice.3), channel_id=1, source_target_pairs={{0,2},{2,0},{1,3},{3,1},{4,6},{6,4},{5,7},{7,5},{8,10},{10,8},{9,1... | collective-permute-start | bytes 737288 | tf_op jit(solution)/shard_map/ppermute | solution.py:331
  4.8 11.0 %collective-permute-start = (s32[2,256]{1,0:T(2,128)}, s32[2,256]{1,0:T(2,128)S(1)}, u32[]{:S(2)}, u32[]{:S(2)}) collective-permute-start(s32[2,256]{1,0:T(2,128)} %bitcast.22), channel_id=1, source_target_pairs={{0,2},{2,0},{1,3},{3,1},{4,6},{6,4},{5,7},{7,5},{8,10},{10,8},{9,1... | collective-permute-start | bytes 6152 | tf_op jit(solution)/shard_map/ppermute | solution.py:329
  7.4 24.0 %all-to-all-start.1 = ((bf16[16,24,1024]{2,1,0:T(8,128)(2,1)}), bf16[16,24,1024]{2,1,0:T(8,128)(2,1)S(1)}, u32[]{:S(2)}, u32[]{:S(2)}) async-start(bf16[16,24,1024]{2,1,0:T(8,128)(2,1)} %bitcast.21), calls=%async_computation.1 | async-start | bytes 1572864 | tf_op jit(solution)/shard_map/all_to_all | solution.py:322
  13.4 15.1 %collective-permute-start.2 = (bf16[136,1024]{1,0:T(8,128)(2,1)}, bf16[136,1024]{1,0:T(8,128)(2,1)S(1)}, u32[]{:S(2)}, u32[]{:S(2)}) collective-permute-start(bf16[136,1024]{1,0:T(8,128)(2,1)} %get-tuple-element.13), channel_id=1, source_target_pairs={{0,2},{2,0},{1,3},{3,1},{4,6},{6,4},{5,7},{7,5},{8,10},{10,8},{9,1... | collective-permute-start | bytes 835592 | tf_op jit(solution)/shard_map/ppermute | solution.py:333
  15.8 0.7 copy-start
  16.5 0.7 copy-start.2
  31.4 17.8 %all-to-all-start = ((bf16[16,24,1024]{2,1,0:T(8,128)(2,1)}), bf16[16,24,1024]{2,1,0:T(8,128)(2,1)S(1)}, u32[]{:S(2)}, u32[]{:S(2)}) async-start(bf16[16,24,1024]{2,1,0:T(8,128)(2,1)} %bitcast.2), calls=%async_computation | async-start | bytes 1572864 | tf_op jit(solution)/shard_map/all_to_all | solution.py:322
  49.2 51.7 %copy-start.1 = (s32[2,256]{1,0:T(2,128)S(1)}, s32[2,256]{1,0:T(2,128)}, u32[]{:S(2)}) copy-start(s32[2,256]{1,0:T(2,128)} %get-tuple-element.10.target_ref) | copy-start | bytes 6148

commit v7 on v6

--- a/solution.py
+++ b/solution.py
@@ -281,11 +281,8 @@
             .reshape(rows, LANES)
             .astype(jnp.bfloat16)
         )
-        for c in range(0, cols, 2):
-            part = jnp.concatenate([column(c), column(c + 1)], axis=1)
-            grad_ref[:, c * LANES : (c + 2) * LANES] = matmul(weight, part, NN).astype(
-                jnp.bfloat16
-            )
+        part = jnp.concatenate([column(c) for c in range(cols)], axis=1)
+        grad_ref[...] = matmul(weight, part, NN).astype(jnp.bfloat16)
     else:
         part = back_ref[:, :width]
         grad_ref[...] = matmul(weight, part, NN).astype(jnp.bfloat16)

time: 103 us -> 103 us (level)
  no operation moved by 1% of the time
where the time goes in v7:
time: 103 us; the launch traced here: 102 us
  blocking collectives  42 us (41%)
  Pallas kernels  24.9 us (24%)
  starting transfers between devices  18.1 us (18%)
  waiting for transfers between devices  14.3 us (14%)
  local copies, waits for them, and re-layouts  2.33 us (2%)
    all_to_all x1, blocking collectives, exchange(): return lax.all_to_all(x, axes, split_axis=0, concat_axis=0, tiled=True)  42 us
    pallas_call x2, Pallas kernels, expert(): pl.pallas_call(functools.partial(expert_body, sizes, packed, int(far)), o...  19.2 us
    all_to_all x2, starting transfers between devices, exchange(): return lax.all_to_all(x, axes, split_axis=0, concat_axis=0, tiled=True)  12.5 us
    ppermute x1, waiting for transfers between devices, per_device(): second = lax.ppermute(late, 'half', swap)  10.6 us
    all_to_all x2, waiting for transfers between devices, exchange(): return lax.all_to_all(x, axes, split_axis=0, concat_axis=0, tiled=True)  3.49 us
    ppermute x1, starting transfers between devices, per_device(): first = lax.ppermute(output_grad[:early], 'half', swap)  3.2 us
    pallas_call x1, Pallas kernels, route(): pl.pallas_call(functools.partial(route_body, experts, per_peer, rest), ou...  2.51 us
    ppermute x1, starting transfers between devices, per_device(): second = lax.ppermute(late, 'half', swap)  2.31 us
  transfers between devices with their start and end apart: 5, of which 4 were waited for; matrix products, arithmetic and copies ran while one was open for 0% of the time, Pallas kernels for 14%

profile of v7, /device:TPU:1, one launch (start us, length us, event | category | flops | bytes accessed | tf_op | source)
XLA Modules:
  0.0 102.3 jit_solution(7597756268308190607)
XLA Ops:
  0.6 1.0 slice.3
  1.6 3.2 %collective-permute-start.1 = (bf16[120,1024]{1,0:T(8,128)(2,1)S(1)}, bf16[120,1024]{1,0:T(8,128)(2,1)S(1)}, u32[]{:S(2)}, u32[]{:S(2)}) collective-permute-start(bf16[120,1024]{1,0:T(8,128)(2,1)S(1)} %slice.3), channel_id=1, source_target_pairs={{0,2},{2,0},{1,3},{3,1},{4,6},{6,4},{5,7},{7,5},{8,10},{10,8},{9,1... | collective-permute-start | bytes 737288 | tf_op jit(solution)/shard_map/ppermute | solution.py:328
  4.8 0.1 collective-permute-start
  4.9 2.5 %route.1 = (bf16[384,1024]{1,0:T(8,128)(2,1)}, s32[2,256]{1,0:T(2,128)}, bf16[136,1024]{1,0:T(8,128)(2,1)}) custom-call(s32[2,256]{1,0:T(2,128)} %bitcast.23, bf16[256,1024]{1,0:T(8,128)(2,1)} %tok_ref.1), custom_call_target="tpu_custom_call" | custom-call | flops 201326592 | bytes 1310720 | tf_op jit(solution)/shard_map/route/pallas_call | solution.py:63
  7.4 6.0 %all-to-all-start.1 = ((bf16[16,24,1024]{2,1,0:T(8,128)(2,1)}), bf16[16,24,1024]{2,1,0:T(8,128)(2,1)S(1)}, u32[]{:S(2)}, u32[]{:S(2)}) async-start(bf16[16,24,1024]{2,1,0:T(8,128)(2,1)} %bitcast.21), calls=%async_computation.1 | async-start | bytes 1572864 | tf_op jit(solution)/shard_map/all_to_all | solution.py:319
  13.4 2.3 %collective-permute-start.2 = (bf16[136,1024]{1,0:T(8,128)(2,1)}, bf16[136,1024]{1,0:T(8,128)(2,1)S(1)}, u32[]{:S(2)}, u32[]{:S(2)}) collective-permute-start(bf16[136,1024]{1,0:T(8,128)(2,1)} %get-tuple-element.13), channel_id=1, source_target_pairs={{0,2},{2,0},{1,3},{3,1},{4,6},{6,4},{5,7},{7,5},{8,10},{10,8},{9,1... | collective-permute-start | bytes 835592 | tf_op jit(solution)/shard_map/ppermute | solution.py:330
  15.7 0.2 collective-permute-done.ids_ref
  15.8 0.0 collective-permute-done.1.tok_ref
  15.8 0.0 copy-start
  15.8 0.7 copy-done
  16.5 0.0 copy-start.2
  16.5 0.7 copy-done.2
  17.2 0.6 gather_first.1
  17.8 10.6 %collective-permute-done.2.tok_ref = bf16[136,1024]{1,0:T(8,128)(2,1)S(1)} collective-permute-done((bf16[136,1024]{1,0:T(8,128)(2,1)}, bf16[136,1024]{1,0:T(8,128)(2,1)S(1)}, u32[]{:S(2)}, u32[]{:S(2)}) %collective-permute-start.2) | collective-permute-done | bytes 278560 | tf_op jit(solution)/shard_map/ppermute | solution.py:330
  28.4 1.3 %gather_last.1 = bf16[384,1024]{1,0:T(8,128)(2,1)} custom-call(bf16[384,136]{1,0:T(8,128)(2,1)S(1)} %get-tuple-element.12.pick_ref, bf16[136,1024]{1,0:T(8,128)(2,1)S(1)} %collective-permute-done.2.tok_ref, bf16[384,1024]{1,0:T(8,128)(2,1)S(1)} %get-tuple-element.14.part_ref), custom_call_target="tpu_custom_call" | custom-call | flops 106954752 | tf_op jit(solution)/shard_map/gather_last/pallas_call | solution.py:116
  29.7 1.7 %all-to-all-done.1 = bf16[16,24,1024]{2,1,0:T(8,128)(2,1)S(1)} async-done(((bf16[16,24,1024]{2,1,0:T(8,128)(2,1)}), bf16[16,24,1024]{2,1,0:T(8,128)(2,1)S(1)}, u32[]{:S(2)}, u32[]{:S(2)}) %all-to-all-start.1) | async-done | bytes 786464 | tf_op jit(solution)/shard_map/all_to_all | solution.py:319
  31.4 6.5 %all-to-all-start = ((bf16[16,24,1024]{2,1,0:T(8,128)(2,1)}), bf16[16,24,1024]{2,1,0:T(8,128)(2,1)S(1)}, u32[]{:S(2)}, u32[]{:S(2)}) async-start(bf16[16,24,1024]{2,1,0:T(8,128)(2,1)} %bitcast.2), calls=%async_computation | async-start | bytes 1572864 | tf_op jit(solution)/shard_map/all_to_all | solution.py:319
  37.9 9.5 %expert_near.1.refs_4_ = bf16[8,2,200,128]{3,2,1,0:T(8,128)(2,1)S(1)} custom-call(bf16[384,1024]{1,0:T(8,128)(2,1)S(1)} %bitcast.12, bf16[8,2,48,4096]{3,2,1,0:T(8,128)(2,1)} %bitcast.19, bf16[4096,1024]{1,0:T(8,128)(2,1)} %bitcast.15, bf16[1024,4096]{1,0:T(8,128)(2,1)} %bitcast.17), custom_call_target="tpu_custom_call" | custom-call | flops 6442450944 | bytes 21495808 | tf_op jit(solution)/shard_map/expert_near/pallas_call | solution.py:230
  47.5 1.7 %all-to-all-done = bf16[16,24,1024]{2,1,0:T(8,128)(2,1)S(1)} async-done(((bf16[16,24,1024]{2,1,0:T(8,128)(2,1)}), bf16[16,24,1024]{2,1,0:T(8,128)(2,1)S(1)}, u32[]{:S(2)}, u32[]{:S(2)}) %all-to-all-start) | async-done | bytes 786464 | tf_op jit(solution)/shard_map/all_to_all | solution.py:319
  49.2 0.0 copy-start.1
  49.2 9.7 %expert_far.1 = bf16[8,2,2,200,128]{4,3,2,1,0:T(8,128)(2,1)S(1)} custom-call(bf16[384,1024]{1,0:T(8,128)(2,1)S(1)} %bitcast.13, bf16[8,2,48,4096]{3,2,1,0:T(8,128)(2,1)} %bitcast.20, bf16[4096,1024]{1,0:T(8,128)(2,1)} %bitcast.16, bf16[1024,4096]{1,0:T(8,128)(2,1)} %bitcast.18, bf16[8,2,200,128]{3,2,1,0:T(8,128)(2,1)S(1)} %expert_near.1.refs_4_), custom_call_target="tpu_custom_call" | custom-call | flops 6442450944 | bytes 21495808 | tf_op jit(solution)/shard_map/expert_far/pallas_call | solution.py:230
  58.9 42.0 %all_to_all.15.back_ref = bf16[32,200,128]{2,1,0:T(8,128)(2,1)S(1)} all-to-all(bf16[32,200,128]{2,1,0:T(8,128)(2,1)S(1)} %bitcast.11), channel_id=1, replica_groups=mesh['outer'=8,'half'=2,'rest'=2] {'outer','half','rest'}, dimensions={0} | all-to-all | bytes 3276800 | tf_op jit(solution)/shard_map/all_to_all | solution.py:319
  100.9 0.0 copy-done.1
  100.9 1.4 %combine.1 = (bf16[256,1024]{1,0:T(8,128)(2,1)}, f32[2,256]{1,0:T(2,128)}) custom-call(s32[2,256]{1,0:T(2,128)S(1)} %copy-done.1, bf16[256,768]{1,0:T(8,128)(2,1)S(1)} %get-tuple-element.11.weight_ref, bf16[32,200,128]{2,1,0:T(8,128)(2,1)S(1)} %all_to_all.15.back_ref), custom_call_target="tpu_custom_call" | custom-call | tf_op jit(solution)/shard_map/combine/pallas_call | solution.py:298
Async XLA Ops:
  1.6 14.2 %collective-permute-start.1 = (bf16[120,1024]{1,0:T(8,128)(2,1)S(1)}, bf16[120,1024]{1,0:T(8,128)(2,1)S(1)}, u32[]{:S(2)}, u32[]{:S(2)}) collective-permute-start(bf16[120,1024]{1,0:T(8,128)(2,1)S(1)} %slice.3), channel_id=1, source_target_pairs={{0,2},{2,0},{1,3},{3,1},{4,6},{6,4},{5,7},{7,5},{8,10},{10,8},{9,1... | collective-permute-start | bytes 737288 | tf_op jit(solution)/shard_map/ppermute | solution.py:328
  4.8 11.0 %collective-permute-start = (s32[2,256]{1,0:T(2,128)}, s32[2,256]{1,0:T(2,128)S(1)}, u32[]{:S(2)}, u32[]{:S(2)}) collective-permute-start(s32[2,256]{1,0:T(2,128)} %bitcast.22), channel_id=1, source_target_pairs={{0,2},{2,0},{1,3},{3,1},{4,6},{6,4},{5,7},{7,5},{8,10},{10,8},{9,1... | collective-permute-start | bytes 6152 | tf_op jit(solution)/shard_map/ppermute | solution.py:326
  7.4 24.0 %all-to-all-start.1 = ((bf16[16,24,1024]{2,1,0:T(8,128)(2,1)}), bf16[16,24,1024]{2,1,0:T(8,128)(2,1)S(1)}, u32[]{:S(2)}, u32[]{:S(2)}) async-start(bf16[16,24,1024]{2,1,0:T(8,128)(2,1)} %bitcast.21), calls=%async_computation.1 | async-start | bytes 1572864 | tf_op jit(solution)/shard_map/all_to_all | solution.py:319
  13.4 15.1 %collective-permute-start.2 = (bf16[136,1024]{1,0:T(8,128)(2,1)}, bf16[136,1024]{1,0:T(8,128)(2,1)S(1)}, u32[]{:S(2)}, u32[]{:S(2)}) collective-permute-start(bf16[136,1024]{1,0:T(8,128)(2,1)} %get-tuple-element.13), channel_id=1, source_target_pairs={{0,2},{2,0},{1,3},{3,1},{4,6},{6,4},{5,7},{7,5},{8,10},{10,8},{9,1... | collective-permute-start | bytes 835592 | tf_op jit(solution)/shard_map/ppermute | solution.py:330
  15.8 0.7 copy-start
  16.5 0.7 copy-start.2
  31.4 17.8 %all-to-all-start = ((bf16[16,24,1024]{2,1,0:T(8,128)(2,1)}), bf16[16,24,1024]{2,1,0:T(8,128)(2,1)S(1)}, u32[]{:S(2)}, u32[]{:S(2)}) async-start(bf16[16,24,1024]{2,1,0:T(8,128)(2,1)} %bitcast.2), calls=%async_computation | async-start | bytes 1572864 | tf_op jit(solution)/shard_map/all_to_all | solution.py:319
  49.2 51.7 %copy-start.1 = (s32[2,256]{1,0:T(2,128)S(1)}, s32[2,256]{1,0:T(2,128)}, u32[]{:S(2)}) copy-start(s32[2,256]{1,0:T(2,128)} %get-tuple-element.10.target_ref) | copy-start | bytes 6148
